TPU v7x, 256 devices: a whole 4x4x8 slice. The times are simulated.
256 devices in a mesh: gx: 16 (over y_lo, z), gy: 16 (over y_hi, x, core).
Axes of the slice: x: 4, y: 4 (y_hi: 2, y_lo: 2; y = y_hi * 2 + y_lo), z: 8, core: 2. Of those that a mesh axis runs over, the one named last changes fastest.
Arguments:
- phase: float32 [256, 512, 256], P('gx', 'gy'), may hold values from -1 to 1
- solute: float32 [256, 512, 256], P('gx', 'gy'), may hold values from -1 to 1
- macro_temp: float32 [64, 128, 64], P('gx', None, 'gy'), may hold values from -1 to 1
Outputs:
- phase_out: float32 [256, 512, 256], P('gx', 'gy')
- solute_out: float32 [256, 512, 256], P('gx', 'gy')
- latent_heat: float32 [64, 128, 64], P('gx', None, 'gy')
All inputs are finite; a program needn't handle non-finite values.
Results may differ from a plain program's by a relative error of at most 0.0001.
Values sent between devices are 32-bit elements; how exact they have to be, the bound alone decides.
A program may use at most 64 MiB of HBM per device.

v0:
```python
import jax
import jax.numpy as jnp
from jax import lax
from jax.sharding import PartitionSpec as P

SUBSTEPS = 2


time_step = 0.1
anisotropy = 0.3
coupling = 2.0
rejection = 0.5


def padded(cells, sides, width):
    for axis, dim in sides:
        count = lax.axis_size(axis)
        head = lax.slice_in_dim(cells, 0, width, axis=dim)
        tail = lax.slice_in_dim(cells, cells.shape[dim] - width, cells.shape[dim], axis=dim)
        cells = jnp.concatenate(
            [
                lax.ppermute(tail, axis, [(i, (i + 1) % count) for i in range(count)]),
                cells,
                lax.ppermute(head, axis, [((i + 1) % count, i) for i in range(count)]),
            ],
            axis=dim,
        )
    return cells


def divergence(pad_field, with_aniso):
    grid = jnp.pad(pad_field, ((0, 0), (0, 0), (2, 2)), mode="edge")
    grad_x = 0.5 * (grid[2:, 1:-1, 1:-1] - grid[:-2, 1:-1, 1:-1])
    grad_y = 0.5 * (grid[1:-1, 2:, 1:-1] - grid[1:-1, :-2, 1:-1])
    grad_z = 0.5 * (grid[1:-1, 1:-1, 2:] - grid[1:-1, 1:-1, :-2])
    if with_aniso:
        sq_x = grad_x * grad_x
        sq_y = grad_y * grad_y
        planar = sq_x + sq_y + 1.0
        factor = 1.0 + anisotropy * (sq_x * sq_x - 6.0 * sq_x * sq_y + sq_y * sq_y) / (
            planar * planar
        )
        stiff = factor * factor
        grad_x = stiff * grad_x
        grad_y = stiff * grad_y
        grad_z = stiff * grad_z
    total = 0.5 * (grad_x[2:, 1:-1, 1:-1] - grad_x[:-2, 1:-1, 1:-1])
    total = total + 0.5 * (grad_y[1:-1, 2:, 1:-1] - grad_y[1:-1, :-2, 1:-1])
    total = total + 0.5 * (grad_z[1:-1, 1:-1, 2:] - grad_z[1:-1, 1:-1, :-2])
    return total


def substep(phase_pad, solute_pad, theta):
    old = phase_pad[2:-2, 2:-2, :]
    conc = solute_pad[2:-2, 2:-2, :]
    square = 1.0 - old * old
    drive = (
        divergence(phase_pad, True)
        + old
        - old * old * old
        - coupling * square * square * (theta + conc)
    )
    new_phase = old + time_step * drive
    new_solute = conc + time_step * divergence(solute_pad, False) + rejection * (new_phase - old)
    return (new_phase, new_solute)


def table(fine, shift, columns):
    lower = jnp.floor_divide(2 * fine - 3, 8)
    frac = (2 * fine - 3 - 8 * lower).astype(jnp.float32) / 8.0
    first = lower + shift
    second = first + 1
    first = jnp.clip(first, 0, columns - 1)
    second = jnp.clip(second, 0, columns - 1)
    ticks = jnp.arange(columns, dtype=jnp.int32)
    lower_hit = (ticks[None, :] == first[:, None]).astype(jnp.float32)
    upper_hit = (ticks[None, :] == second[:, None]).astype(jnp.float32)
    return (1.0 - frac)[:, None] * lower_hit + frac[:, None] * upper_hit


def body(phase, solute, macro_temp):
    cells_x, cells_y, cells_z = phase.shape
    margin = 0
    fine_x = jnp.arange(cells_x + 2 * margin, dtype=jnp.int32) - margin
    fine_y = jnp.arange(cells_y + 2 * margin, dtype=jnp.int32) - margin
    fine_z = jnp.arange(cells_z, dtype=jnp.int32)
    swapped = lax.all_to_all(macro_temp, "gy", split_axis=1, concat_axis=2, tiled=True)
    framed = padded(swapped, (("gx", 0), ("gy", 1)), 1)
    x_table = table(fine_x, 1, framed.shape[0])
    y_table = table(fine_y, 1, framed.shape[1])
    z_table = table(fine_z, 0, framed.shape[2])
    highest = lax.Precision.HIGHEST
    theta = jnp.einsum("fk,kyz->fyz", x_table, framed, precision=highest)
    theta = jnp.einsum("gk,fkz->fgz", y_table, theta, precision=highest)
    theta = jnp.einsum("hk,fgk->fgh", z_table, theta, precision=highest)
    current_phase, current_solute = (phase, solute)
    for step in range(SUBSTEPS):
        extended = padded(jnp.stack([current_phase, current_solute]), (("gx", 1), ("gy", 2)), 2)
        current_phase, current_solute = substep(extended[0], extended[1], theta)
    change = 0.5 * (current_phase - phase)
    restricted = change.reshape(cells_x // 4, 4, cells_y // 4, 4, cells_z // 4, 4).mean(
        axis=(1, 3, 5)
    )
    latent = lax.all_to_all(restricted, "gy", split_axis=2, concat_axis=1, tiled=True)
    return (current_phase, current_solute, latent)


def solution(mesh):
    in_specs = (P("gx", "gy", None), P("gx", "gy", None), P("gx", None, "gy"))
    out_specs = (P("gx", "gy", None), P("gx", "gy", None), P("gx", None, "gy"))
    return jax.shard_map(body, mesh=mesh, in_specs=in_specs, out_specs=out_specs, check_vma=False)
```

profile of v0, /device:TPU:1, one launch (start us, length us, event | category | flops | bytes accessed | tf_op | source)
XLA Modules:
  0.0 127.0 jit_solution(8066457896767869592)
XLA Ops:
  2.4 8.4 %all-to-all-start = ((f32[16,1,128]{2,1,0:T(1,128)}), f32[16,1,128]{2,1,0:T(1,128)S(1)}, u32[]{:S(2)}, u32[]{:S(2)}) async-start(f32[16,1,128]{2,1,0:T(1,128)} %reshape.169), calls=%async_computation | async-start | bytes 16384 | tf_op jit(solution)/shard_map/all_to_all | solution.py:87
  11.8 1.7 %collective-permute-start = (f32[2,2,32,256]{3,2,1,0:T(8,128)S(1)}, f32[2,2,32,256]{3,2,1,0:T(8,128)S(1)}, u32[]{:S(2)}, u32[]{:S(2)}) collective-permute-start(f32[2,2,32,256]{3,2,1,0:T(8,128)S(1)} %get-tuple-element.37), channel_id=1, source_target_pairs={{0,16},{16,32},{32,48},{48,64},{64,80},{80,96},{96,112},{112,128},... | collective-permute-start | bytes 393224 | tf_op jit(solution)/shard_map/ppermute | solution.py:22
  13.5 4.1 %collective-permute-start.1 = (f32[2,2,32,256]{3,2,1,0:T(8,128)S(1)}, f32[2,2,32,256]{3,2,1,0:T(8,128)S(1)}, u32[]{:S(2)}, u32[]{:S(2)}) collective-permute-start(f32[2,2,32,256]{3,2,1,0:T(8,128)S(1)} %get-tuple-element.38), channel_id=1, source_target_pairs={{16,0},{32,16},{48,32},{64,48},{80,64},{96,80},{112,96},{128,112},... | collective-permute-start | bytes 393224 | tf_op jit(solution)/shard_map/ppermute | solution.py:24
  19.9 5.8 %collective-permute-start.5 = (f32[1,8,64]{1,2,0:T(8,128)S(1)}, f32[1,8,64]{1,2,0:T(8,128)S(1)}, u32[]{:S(2)}, u32[]{:S(2)}) collective-permute-start(f32[1,8,64]{1,2,0:T(8,128)S(1)} %bitcast.59), channel_id=1, source_target_pairs={{16,0},{32,16},{48,32},{64,48},{80,64},{96,80},{112,96},{128,112},... | collective-permute-start | bytes 6152 | tf_op jit(solution)/shard_map/ppermute | solution.py:24
  26.6 3.9 %collective-permute-done.4 = f32[1,8,64]{1,2,0:T(8,128)S(1)} collective-permute-done((f32[1,8,64]{1,2,0:T(8,128)S(1)}, f32[1,8,64]{1,2,0:T(8,128)S(1)}, u32[]{:S(2)}, u32[]{:S(2)}) %collective-permute-start.4) | collective-permute-done | bytes 2080 | tf_op jit(solution)/shard_map/ppermute | solution.py:22
  30.6 2.3 %collective-permute-start.6 = (f32[6,1,64]{1,2,0:T(8,128)S(1)}, f32[6,1,64]{1,2,0:T(8,128)S(1)}, u32[]{:S(2)}, u32[]{:S(2)}) collective-permute-start(f32[6,1,64]{1,2,0:T(8,128)S(1)} %get-tuple-element.39), channel_id=1, source_target_pairs={{0,1},{1,2},{2,3},{3,4},{4,5},{5,6},{6,7},{7,8},{8,9},{9,10},{10,1... | collective-permute-start | bytes 4616 | tf_op jit(solution)/shard_map/ppermute | solution.py:22
  33.1 2.5 %collective-permute-done.6 = f32[6,1,64]{1,2,0:T(8,128)S(1)} collective-permute-done((f32[6,1,64]{1,2,0:T(8,128)S(1)}, f32[6,1,64]{1,2,0:T(8,128)S(1)}, u32[]{:S(2)}, u32[]{:S(2)}) %collective-permute-start.6) | collective-permute-done | bytes 1568 | tf_op jit(solution)/shard_map/ppermute | solution.py:22
  35.7 2.4 %collective-permute-done.7 = f32[6,1,64]{1,2,0:T(8,128)S(1)} collective-permute-done((f32[6,1,64]{1,2,0:T(8,128)S(1)}, f32[6,1,64]{1,2,0:T(8,128)S(1)}, u32[]{:S(2)}, u32[]{:S(2)}) %collective-permute-start.7) | collective-permute-done | bytes 1568 | tf_op jit(solution)/shard_map/ppermute | solution.py:24
  39.2 3.7 %collective-permute-start.3 = (f32[2,20,2,256]{3,2,1,0:T(2,128)S(1)}, f32[2,20,2,256]{3,2,1,0:T(2,128)S(1)}, u32[]{:S(2)}, u32[]{:S(2)}) collective-permute-start(f32[2,20,2,256]{3,2,1,0:T(2,128)S(1)} %get-tuple-element.26), channel_id=1, source_target_pairs={{1,0},{2,1},{3,2},{4,3},{5,4},{6,5},{7,6},{8,7},{9,8},{10,9},{11,1... | collective-permute-start | bytes 245768 | tf_op jit(solution)/shard_map/ppermute | solution.py:24
  48.4 1.3 fusion.47
  50.7 1.7 %fusion.41 = (f32[1,16,32,256]{3,2,1,0:T(8,128)S(1)}, f32[16,32,256]{2,1,0:T(8,128)S(1)}) fusion(f32[18,34,258]{2,1,0:T(8,128)S(1)} %fusion.10, f32[18,34,258]{2,1,0:T(8,128)S(1)} %get-tuple-element.30, f32[18,34,258]{2,1,0:T(8,128)S(1)} %get-tuple-element.29, f32[20,36,256]{2,1,0:T(8,128)S(1)} %get-tuple-element.22, ...), kind=kLoop, calls=%fused_computation.83 | loop fusion | flops 3670016 | bytes 8912896 | tf_op jit(solution)/shard_map/stack | solution.py:98
  52.6 3.6 %collective-permute-start.9 = (f32[2,2,32,256]{3,2,1,0:T(8,128)S(1)}, f32[2,2,32,256]{3,2,1,0:T(8,128)S(1)}, u32[]{:S(2)}, u32[]{:S(2)}) collective-permute-start(f32[2,2,32,256]{3,2,1,0:T(8,128)S(1)} %get-tuple-element.36), channel_id=1, source_target_pairs={{16,0},{32,16},{48,32},{64,48},{80,64},{96,80},{112,96},{128,112},... | collective-permute-start | bytes 393224 | tf_op jit(solution)/shard_map/ppermute | solution.py:24
  56.1 2.4 %collective-permute-done.8 = f32[2,2,32,256]{3,2,1,0:T(8,128)S(1)} collective-permute-done((f32[2,2,32,256]{3,2,1,0:T(8,128)S(1)}, f32[2,2,32,256]{3,2,1,0:T(8,128)S(1)}, u32[]{:S(2)}, u32[]{:S(2)}) %collective-permute-start.8) | collective-permute-done | bytes 131104 | tf_op jit(solution)/shard_map/ppermute | solution.py:22
  58.6 1.7 %collective-permute-start.10 = (f32[2,20,2,256]{3,2,1,0:T(2,128)S(1)}, f32[2,20,2,256]{3,2,1,0:T(2,128)S(1)}, u32[]{:S(2)}, u32[]{:S(2)}) collective-permute-start(f32[2,20,2,256]{3,2,1,0:T(2,128)S(1)} %get-tuple-element.23), channel_id=1, source_target_pairs={{0,1},{1,2},{2,3},{3,4},{4,5},{5,6},{6,7},{7,8},{8,9},{9,10},{10,1... | collective-permute-start | bytes 245768 | tf_op jit(solution)/shard_map/ppermute | solution.py:22
  60.3 6.2 %collective-permute-start.11 = (f32[2,20,2,256]{3,2,1,0:T(2,128)S(1)}, f32[2,20,2,256]{3,2,1,0:T(2,128)S(1)}, u32[]{:S(2)}, u32[]{:S(2)}) collective-permute-start(f32[2,20,2,256]{3,2,1,0:T(2,128)S(1)} %get-tuple-element.24), channel_id=1, source_target_pairs={{1,0},{2,1},{3,2},{4,3},{5,4},{6,5},{7,6},{8,7},{9,8},{10,9},{11,1... | collective-permute-start | bytes 245768 | tf_op jit(solution)/shard_map/ppermute | solution.py:24
  68.5 1.5 %fusion.1 = f32[18,34,258]{2,1,0:T(8,128)} fusion(f32[20,36,256]{2,1,0:T(8,128)S(1)} %get-tuple-element.20, f32[20,36,2]{2,1,0:T(8,128)S(1)} %reshape.155, f32[20,36,2]{2,1,0:T(8,128)S(1)} %reshape.156), kind=kLoop, calls=%fused_computation.9 | loop fusion | flops 631584 | bytes 1380384 | tf_op jit(solution)/shard_map/mul | solution.py:35
  70.9 2.2 %fusion.3 = (f32[18,34,258]{2,1,0:T(8,128)S(1)}, f32[18,34,258]{2,1,0:T(8,128)}) fusion(f32[20,36,260]{2,1,0:T(8,128)S(1)} %pad_maximum_fusion.5), kind=kLoop, calls=%fused_computation.14 | loop fusion | flops 631584 | bytes 3789504 | tf_op jit(solution)/shard_map/mul | solution.py:33
  73.9 1.3 fusion.49
  76.2 1.9 %subtract_multiply_fusion = (f32[16,32,256]{2,1,0:T(8,128)}, f32[16,32,256]{2,1,0:T(8,128)}) fusion(f32[16,32,256]{2,1,0:T(8,128)S(1)} %copy-done, f32[16,32,256]{2,1,0:T(8,128)S(1)} %fusion.52, f32[20,36,256]{2,1,0:T(8,128)S(1)} %get-tuple-element.20, f32[18,34,258]{2,1,0:T(8,128)S(1)} %get-tuple-element.32, f32[18,34,258]{2,1,0:T(8,128)S(1)} %get-tuple-element.31, ...), kind=kLoop, calls=%fused_computation.94 | loop fusion | flops 2621440 | bytes 6291456 | tf_op jit(solution)/shard_map/mul | solution.py:100
  78.1 19.5 %reshape.157 = f32[4,4,8,4,64,4]{5,4,3,2,1,0:T(8,128)} reshape(f32[16,32,256]{2,1,0:T(8,128)} %get-tuple-element.11) | data formatting | bytes 1048576 | tf_op jit(solution)/shard_map/reshape | solution.py:101
  97.6 7.1 %reduce_sum.9 = f32[4,8,64]{2,1,0:T(8,128)S(1)} reduce(f32[4,4,8,4,64,4]{5,4,3,2,1,0:T(8,128)} %reshape.157, f32[]{:T(128)} %constant.93.clone.1), dimensions={1,3,5}, to_apply=%region_0.1 | reduce | flops 129024 | bytes 532484 | tf_op jit(solution)/shard_map/reduce_sum | solution.py:101
  105.6 12.9 %all-to-all-start.1 = ((f32[16,1,128]{2,1,0:T(1,128)}), f32[16,1,128]{2,1,0:T(1,128)S(1)}, u32[]{:S(2)}, u32[]{:S(2)}) async-start(f32[16,1,128]{2,1,0:T(1,128)} %reshape.171), calls=%async_computation.1 | async-start | bytes 16384 | tf_op jit(solution)/shard_map/all_to_all | solution.py:104
  118.5 3.5 %fusion.31 = f32[16,32,256]{2,1,0:T(8,128)} fusion(f32[18,34,258]{2,1,0:T(8,128)} %fusion.1, f32[18,34,258]{2,1,0:T(8,128)} %get-tuple-element.28, f32[18,34,258]{2,1,0:T(8,128)S(1)} %get-tuple-element.27, f32[16,32,256]{2,1,0:T(8,128)S(1)} %copy-done.2, f32[20,36,256]{2,1,0:T(8,128)S(1)} %get-tuple-element.20, f32[20,36,256]{2,1,0:T(8,128)S(1)} %get-tuple-element.19), kind=kLoop, calls=%fused_computation.67 | loop fusion | flops 1310720 | bytes 5242880 | tf_op jit(solution)/shard_map/add | solution.py:64
  122.0 3.4 %all-to-all-done.1 = f32[16,1,128]{2,1,0:T(1,128)S(1)} async-done(((f32[16,1,128]{2,1,0:T(1,128)}), f32[16,1,128]{2,1,0:T(1,128)S(1)}, u32[]{:S(2)}, u32[]{:S(2)}) %all-to-all-start.1) | async-done | bytes 8224 | tf_op jit(solution)/shard_map/all_to_all | solution.py:104
  (78 shorter events, 21.1 us)
Async XLA Ops:
  2.4 15.4 %all-to-all-start = ((f32[16,1,128]{2,1,0:T(1,128)}), f32[16,1,128]{2,1,0:T(1,128)S(1)}, u32[]{:S(2)}, u32[]{:S(2)}) async-start(f32[16,1,128]{2,1,0:T(1,128)} %reshape.169), calls=%async_computation | async-start | bytes 16384 | tf_op jit(solution)/shard_map/all_to_all | solution.py:87
  11.8 27.1 %collective-permute-start = (f32[2,2,32,256]{3,2,1,0:T(8,128)S(1)}, f32[2,2,32,256]{3,2,1,0:T(8,128)S(1)}, u32[]{:S(2)}, u32[]{:S(2)}) collective-permute-start(f32[2,2,32,256]{3,2,1,0:T(8,128)S(1)} %get-tuple-element.37), channel_id=1, source_target_pairs={{0,16},{16,32},{32,48},{48,64},{64,80},{80,96},{96,112},{112,128},... | collective-permute-start | bytes 393224 | tf_op jit(solution)/shard_map/ppermute | solution.py:22
  13.5 25.4 %collective-permute-start.1 = (f32[2,2,32,256]{3,2,1,0:T(8,128)S(1)}, f32[2,2,32,256]{3,2,1,0:T(8,128)S(1)}, u32[]{:S(2)}, u32[]{:S(2)}) collective-permute-start(f32[2,2,32,256]{3,2,1,0:T(8,128)S(1)} %get-tuple-element.38), channel_id=1, source_target_pairs={{16,0},{32,16},{48,32},{64,48},{80,64},{96,80},{112,96},{128,112},... | collective-permute-start | bytes 393224 | tf_op jit(solution)/shard_map/ppermute | solution.py:24
  19.9 6.8 %collective-permute-start.5 = (f32[1,8,64]{1,2,0:T(8,128)S(1)}, f32[1,8,64]{1,2,0:T(8,128)S(1)}, u32[]{:S(2)}, u32[]{:S(2)}) collective-permute-start(f32[1,8,64]{1,2,0:T(8,128)S(1)} %bitcast.59), channel_id=1, source_target_pairs={{16,0},{32,16},{48,32},{64,48},{80,64},{96,80},{112,96},{128,112},... | collective-permute-start | bytes 6152 | tf_op jit(solution)/shard_map/ppermute | solution.py:24
  25.6 4.9 %collective-permute-start.4 = (f32[1,8,64]{1,2,0:T(8,128)S(1)}, f32[1,8,64]{1,2,0:T(8,128)S(1)}, u32[]{:S(2)}, u32[]{:S(2)}) collective-permute-start(f32[1,8,64]{1,2,0:T(8,128)S(1)} %bitcast.58), channel_id=1, source_target_pairs={{0,16},{16,32},{32,48},{48,64},{64,80},{80,96},{96,112},{112,128},... | collective-permute-start | bytes 6152 | tf_op jit(solution)/shard_map/ppermute | solution.py:22
  30.5 8.4 %copy-start = (f32[16,32,256]{2,1,0:T(8,128)S(1)}, f32[16,32,256]{2,1,0:T(8,128)}, u32[]{:S(2)}) copy-start(f32[16,32,256]{2,1,0:T(8,128)} %param.3) | copy-start | bytes 1572868
  30.5 8.4 %copy-start.1 = (f32[16,32,256]{2,1,0:T(8,128)S(1)}, f32[16,32,256]{2,1,0:T(8,128)}, u32[]{:S(2)}) copy-start(f32[16,32,256]{2,1,0:T(8,128)} %param.4) | copy-start | bytes 1572868
  30.6 5.0 %collective-permute-start.6 = (f32[6,1,64]{1,2,0:T(8,128)S(1)}, f32[6,1,64]{1,2,0:T(8,128)S(1)}, u32[]{:S(2)}, u32[]{:S(2)}) collective-permute-start(f32[6,1,64]{1,2,0:T(8,128)S(1)} %get-tuple-element.39), channel_id=1, source_target_pairs={{0,1},{1,2},{2,3},{3,4},{4,5},{5,6},{6,7},{7,8},{8,9},{9,10},{10,1... | collective-permute-start | bytes 4616 | tf_op jit(solution)/shard_map/ppermute | solution.py:22
  33.0 5.1 %collective-permute-start.7 = (f32[6,1,64]{1,2,0:T(8,128)S(1)}, f32[6,1,64]{1,2,0:T(8,128)S(1)}, u32[]{:S(2)}, u32[]{:S(2)}) collective-permute-start(f32[6,1,64]{1,2,0:T(8,128)S(1)} %get-tuple-element.40), channel_id=1, source_target_pairs={{1,0},{2,1},{3,2},{4,3},{5,4},{6,5},{7,6},{8,7},{9,8},{10,9},{11,1... | collective-permute-start | bytes 4616 | tf_op jit(solution)/shard_map/ppermute | solution.py:24
  39.0 4.5 %collective-permute-start.2 = (f32[2,20,2,256]{3,2,1,0:T(2,128)S(1)}, f32[2,20,2,256]{3,2,1,0:T(2,128)S(1)}, u32[]{:S(2)}, u32[]{:S(2)}) collective-permute-start(f32[2,20,2,256]{3,2,1,0:T(2,128)S(1)} %get-tuple-element.25), channel_id=1, source_target_pairs={{0,1},{1,2},{2,3},{3,4},{4,5},{5,6},{6,7},{7,8},{8,9},{9,10},{10,1... | collective-permute-start | bytes 245768 | tf_op jit(solution)/shard_map/ppermute | solution.py:22
  39.2 4.6 %collective-permute-start.3 = (f32[2,20,2,256]{3,2,1,0:T(2,128)S(1)}, f32[2,20,2,256]{3,2,1,0:T(2,128)S(1)}, u32[]{:S(2)}, u32[]{:S(2)}) collective-permute-start(f32[2,20,2,256]{3,2,1,0:T(2,128)S(1)} %get-tuple-element.26), channel_id=1, source_target_pairs={{1,0},{2,1},{3,2},{4,3},{5,4},{6,5},{7,6},{8,7},{9,8},{10,9},{11,1... | collective-permute-start | bytes 245768 | tf_op jit(solution)/shard_map/ppermute | solution.py:24
  52.5 6.0 %collective-permute-start.8 = (f32[2,2,32,256]{3,2,1,0:T(8,128)S(1)}, f32[2,2,32,256]{3,2,1,0:T(8,128)S(1)}, u32[]{:S(2)}, u32[]{:S(2)}) collective-permute-start(f32[2,2,32,256]{3,2,1,0:T(8,128)S(1)} %get-tuple-element.35), channel_id=1, source_target_pairs={{0,16},{16,32},{32,48},{48,64},{64,80},{80,96},{96,112},{112,128},... | collective-permute-start | bytes 393224 | tf_op jit(solution)/shard_map/ppermute | solution.py:22
  52.6 5.9 %collective-permute-start.9 = (f32[2,2,32,256]{3,2,1,0:T(8,128)S(1)}, f32[2,2,32,256]{3,2,1,0:T(8,128)S(1)}, u32[]{:S(2)}, u32[]{:S(2)}) collective-permute-start(f32[2,2,32,256]{3,2,1,0:T(8,128)S(1)} %get-tuple-element.36), channel_id=1, source_target_pairs={{16,0},{32,16},{48,32},{64,48},{80,64},{96,80},{112,96},{128,112},... | collective-permute-start | bytes 393224 | tf_op jit(solution)/shard_map/ppermute | solution.py:24
  58.6 8.4 %collective-permute-start.10 = (f32[2,20,2,256]{3,2,1,0:T(2,128)S(1)}, f32[2,20,2,256]{3,2,1,0:T(2,128)S(1)}, u32[]{:S(2)}, u32[]{:S(2)}) collective-permute-start(f32[2,20,2,256]{3,2,1,0:T(2,128)S(1)} %get-tuple-element.23), channel_id=1, source_target_pairs={{0,1},{1,2},{2,3},{3,4},{4,5},{5,6},{6,7},{7,8},{8,9},{9,10},{10,1... | collective-permute-start | bytes 245768 | tf_op jit(solution)/shard_map/ppermute | solution.py:22
  60.3 7.1 %collective-permute-start.11 = (f32[2,20,2,256]{3,2,1,0:T(2,128)S(1)}, f32[2,20,2,256]{3,2,1,0:T(2,128)S(1)}, u32[]{:S(2)}, u32[]{:S(2)}) collective-permute-start(f32[2,20,2,256]{3,2,1,0:T(2,128)S(1)} %get-tuple-element.24), channel_id=1, source_target_pairs={{1,0},{2,1},{3,2},{4,3},{5,4},{6,5},{7,6},{8,7},{9,8},{10,9},{11,1... | collective-permute-start | bytes 245768 | tf_op jit(solution)/shard_map/ppermute | solution.py:24
  97.6 20.9 %copy-start.2 = (f32[16,32,256]{2,1,0:T(8,128)S(1)}, f32[16,32,256]{2,1,0:T(8,128)}, u32[]{:S(2)}) copy-start(f32[16,32,256]{2,1,0:T(8,128)} %get-tuple-element.12) | copy-start | bytes 1572868
  105.6 19.8 %all-to-all-start.1 = ((f32[16,1,128]{2,1,0:T(1,128)}), f32[16,1,128]{2,1,0:T(1,128)S(1)}, u32[]{:S(2)}, u32[]{:S(2)}) async-start(f32[16,1,128]{2,1,0:T(1,128)} %reshape.171), calls=%async_computation.1 | async-start | bytes 16384 | tf_op jit(solution)/shard_map/all_to_all | solution.py:104
where the time goes:
time: 127 us
  starting transfers between devices  50.8 us (40%)
  other arithmetic  29.1 us (23%)
  local copies, waits for them, and re-layouts  28.1 us (22%)
  waiting for transfers between devices  16.7 us (13%)
  matrix products  1.27 us (1%)
    ppermute x6, starting transfers between devices, padded(): lax.ppermute(head, axis, [((i + 1) % count, i) for i in range(count)])  23.4 us
    reshape x1, local copies, waits for them, and re-layouts, body(): change.reshape(cells_x // 4, 4, cells_y // 4, 4, cells_z // 4, 4)  19.5 us
    all_to_all x1, starting transfers between devices, body(): lax.all_to_all(restricted, 'gy', split_axis=2, concat_axis=1, tiled=True)  12.9 us
    ppermute x6, waiting for transfers between devices, padded(): lax.ppermute(tail, axis, [(i, (i + 1) % count) for i in range(count)])  9.15 us
    all_to_all x1, starting transfers between devices, body(): lax.all_to_all(macro_temp, 'gy', split_axis=1, concat_axis=2, tiled=True)  8.45 us
    reduce_sum x1, other arithmetic, body(): change.reshape(cells_x // 4, 4, cells_y // 4, 4, cells_z // 4, 4)  7.1 us
    ppermute x6, starting transfers between devices, padded(): lax.ppermute(tail, axis, [(i, (i + 1) % count) for i in range(count)])  6.09 us
    ppermute x6, waiting for transfers between devices, padded(): lax.ppermute(head, axis, [((i + 1) % count, i) for i in range(count)])  4.11 us
  transfers between devices with their start and end apart: 14, of which 9 were waited for; matrix products, arithmetic and copies ran while one was open for 7% of the time, Pallas kernels for 0%

commit v1 on v0

v1 whole, which is shorter than its diff:
```python
import functools

import jax
import jax.numpy as jnp
import numpy as np
from jax import lax
from jax.experimental import pallas as pl
from jax.experimental.pallas import tpu as pltpu
from jax.sharding import PartitionSpec as P

MESH = pl.DeviceIdType.MESH
HIGHEST = lax.Precision.HIGHEST

BX, BY = 16, 32
M = 4
EX = BX + 2 * M
RY = 8
EY = 48
LANES = 128
ROWS = (4, 12, 20, 28, 36)
OWN = (8, 16, 24, 32)


def tables(parts):
    wy = np.zeros((128, 4 * LANES), np.float32)
    for row in range(40):
        y = row - 4
        low = (2 * y - 3) // 8
        frac = (2 * y - 3 - 8 * low) / 8.0
        for hit, weight in ((low + 1, 1.0 - frac), (low + 2, frac)):
            if 0 <= hit < 10:
                for z in range(4):
                    wy[32 * z + hit, LANES * z + row] += weight
    wz = np.zeros((64, 256), np.float32)
    for fine in range(256):
        low = (2 * fine - 3) // 8
        frac = (2 * fine - 3 - 8 * low) / 8.0
        for hit, weight in ((low, 1.0 - frac), (low + 1, frac)):
            hit = min(max(hit, 0), 63)
            wz[16 * (hit % 4) + hit // 4, fine] += weight
    py = np.zeros((32, 32), np.float32)
    for y in range(32):
        py[y // 4, y] = 1.0
    pz = np.zeros((64, 256), np.float32)
    for fine in range(256):
        z = fine // 4
        pz[16 * (z % 4) + z // 4, fine] = 1.0 / 128.0
    return wy, wz, py, pz


def kernel(nx, ny, p_in, c_in, m_in, wy_in, wz_in, py_in, pz_in, p_out, c_out, lat_out,
           p0, c0, p1, c1, fx, fy, fz, th, p2, c2, lat, wy, wz, py, pz, mac, s1, r1, xs, xr, s2, r2, lat_v,
           load_sem, out_sem, x_send, x_recv, y_send, y_recv, d_send, d_recv, t_send, t_recv, h_send, h_recv, l_send, l_recv):
    a = lax.axis_index("gx")
    b = lax.axis_index("gy")
    up_x, down_x = lax.rem(a + 1, nx), lax.rem(a + nx - 1, nx)
    up_y, down_y = lax.rem(b + 1, ny), lax.rem(b + ny - 1, ny)

    own = slice(M, M + BX)
    loads = []
    for f, (src, dst) in enumerate(((p_in, p0), (c_in, c0))):
        for h in range(2):
            loads.append(pltpu.make_async_copy(
                src.at[:, :, pl.ds(h * LANES, LANES)],
                dst.at[h, pl.ds(M, BX), pl.ds(RY, BY), :],
                load_sem.at[2 * f + h]))
    for k, (src, dst) in enumerate(((m_in, mac), (wy_in, wy), (wz_in, wz), (py_in, py), (pz_in, pz))):
        loads.append(pltpu.make_async_copy(src, dst, load_sem.at[4 + k]))
    loads[4].start()
    for copy in loads[:4] + loads[5:]:
        copy.start()

    barrier = pltpu.get_barrier_semaphore()
    corners = ((up_x, up_y), (up_x, down_y), (down_x, up_y), (down_x, down_y))
    peers = [(up_x, b), (down_x, b)] + list(corners)
    for k in range(1, ny):
        peers.append((a, lax.rem(b + k, ny)))
    for peer in peers:
        pl.semaphore_signal(barrier, inc=1, device_id=peer, device_id_type=MESH)

    lane = lax.broadcasted_iota(jnp.int32, (8, LANES), 1)
    first, last = lane == 0, lane == LANES - 1
    first2, last2 = lane < 2, lane >= LANES - 2

    loads[4].wait()
    lane4 = lax.broadcasted_iota(jnp.int32, (4, LANES), 1)
    zone = lane4 // 32
    layers = [mac[pl.ds(z, 4, stride=4), :] for z in range(4)]
    for dest in range(16):
        parts = [pltpu.roll(layers[z], (32 * z - 8 * dest + 1) % LANES, 1) for z in range(4)]
        tile = jnp.where(zone == 0, parts[0], jnp.where(zone == 1, parts[1], jnp.where(zone == 2, parts[2], parts[3])))
        s1[pl.ds(8 * dest, 4), :] = tile

    for copy in loads[:4]:
        copy.wait()
    pl.semaphore_wait(barrier, len(peers))

    x_copies, y_copies, d_copies = [], [], []
    lo, hi = pl.ds(M, M), pl.ds(BX, M)
    before, after = pl.ds(0, M), pl.ds(M + BX, M)
    row_lo, row_hi = pl.ds(RY, M), pl.ds(RY + BY - M, M)
    row_before, row_after = pl.ds(RY - M, M), pl.ds(RY + BY, M)
    rows, planes = pl.ds(RY, BY), pl.ds(M, BX)

    def remote(src, dst, send, recv, peer):
        return pltpu.make_async_remote_copy(
            src_ref=src, dst_ref=dst, send_sem=send, recv_sem=recv, device_id=peer, device_id_type=MESH)

    for f, field in enumerate((p0, c0)):
        for side, (src, dst, peer) in enumerate(((hi, before, (up_x, b)), (lo, after, (down_x, b)))):
            k = 2 * f + side
            x_copies.append(remote(field.at[:, src, rows, :], field.at[:, dst, rows, :], x_send.at[k], x_recv.at[k], peer))
        for side, (src, dst, peer) in enumerate(((row_hi, row_before, (a, up_y)), (row_lo, row_after, (a, down_y)))):
            k = 2 * f + side
            y_copies.append(remote(field.at[:, planes, src, :], field.at[:, planes, dst, :], y_send.at[k], y_recv.at[k], peer))
        for side, (sx, dx, sy, dy, peer) in enumerate((
            (hi, before, row_hi, row_before, corners[0]),
            (hi, before, row_lo, row_after, corners[1]),
            (lo, after, row_hi, row_before, corners[2]),
            (lo, after, row_lo, row_after, corners[3]),
        )):
            k = 4 * f + side
            d_copies.append(remote(field.at[:, sx, sy, :], field.at[:, dx, dy, :], d_send.at[k], d_recv.at[k], peer))
    for copy in x_copies + y_copies:
        copy.start()

    def exchange(src, dst, send, recv):
        out = []
        for k in range(1, ny):
            to = lax.rem(b + k, ny)
            out.append(remote(
                src.at[pl.ds(pl.multiple_of(8 * to, 8), 8), :], dst.at[pl.ds(pl.multiple_of(8 * b, 8), 8), :],
                send.at[k], recv.at[k], (a, to)))
        return out

    here = pl.ds(pl.multiple_of(8 * b, 8), 8)
    t_copies = exchange(s1, r1, t_send, t_recv)
    for copy in t_copies:
        copy.start()
    for copy in d_copies:
        copy.start()
    r1[here, :] = s1[here, :]
    for copy in t_copies:
        copy.wait_recv()
    xs[0] = r1[pl.ds(3, 16, stride=8), :]
    xs[1] = r1[pl.ds(0, 16, stride=8), :]
    h_copies = [remote(xs.at[0], xr.at[0], h_send.at[0], h_recv.at[0], (up_x, b)),
                remote(xs.at[1], xr.at[1], h_send.at[1], h_recv.at[1], (down_x, b))]
    for copy in h_copies:
        copy.start()

    def flux(p, e):
        for r in ROWS:
            at = pl.ds(r, 8)
            v = [p[h, e, at, :] for h in range(2)]
            fwd = [pltpu.roll(v[h], 1, 1) for h in range(2)]
            bwd = [pltpu.roll(v[h], LANES - 1, 1) for h in range(2)]
            gz = [jnp.where(last, bwd[1], bwd[0]) - jnp.where(first, v[0], fwd[0]),
                  jnp.where(last, v[1], bwd[1]) - jnp.where(first, fwd[0], fwd[1])]
            wz_ = []
            for h in range(2):
                gx = p[h, e + 1, at, :] - p[h, e - 1, at, :]
                gy = p[h, e, pl.ds(r + 1, 8), :] - p[h, e, pl.ds(r - 1, 8), :]
                sx, sy = gx * gx, gy * gy
                total = sx + sy
                planar = total + 4.0
                ratio = (total * total - 8.0 * (sx * sy)) / (planar * planar)
                factor = 1.0 + 0.3 * ratio
                stiff = factor * factor
                fx[h, e, at, :] = stiff * gx
                fy[h, e, at, :] = stiff * gy
                wz_.append(stiff * gz[h])
            fwd = [pltpu.roll(w, 1, 1) for w in wz_]
            bwd = [pltpu.roll(w, LANES - 1, 1) for w in wz_]
            fz[0, e, at, :] = jnp.where(last, bwd[1], bwd[0]) - jnp.where(first, 0.0, fwd[0])
            fz[1, e, at, :] = jnp.where(last, 0.0, bwd[1]) - jnp.where(first, fwd[0], fwd[1])

    def update(p, c, e, r, theta, store):
        at = pl.ds(r, 8)
        v = [c[h, e, at, :] for h in range(2)]
        fwd = [pltpu.roll(v[h], 2, 1) for h in range(2)]
        bwd = [pltpu.roll(v[h], LANES - 2, 1) for h in range(2)]
        head = jnp.where(first, v[0], pltpu.roll(v[0], 1, 1))
        tail = jnp.where(last, v[1], pltpu.roll(v[1], LANES - 1, 1))
        lz = [jnp.where(last2, bwd[1], bwd[0]) + jnp.where(first2, head, fwd[0]),
              jnp.where(last2, tail, bwd[1]) + jnp.where(first2, fwd[0], fwd[1])]
        for h in range(2):
            div = (fx[h, e + 1, at, :] - fx[h, e - 1, at, :]
                   + (fy[h, e, pl.ds(r + 1, 8), :] - fy[h, e, pl.ds(r - 1, 8), :]) + fz[h, e, at, :])
            old = p[h, e, at, :]
            conc = v[h]
            square = 1.0 - old * old
            step = square * (0.1 * old - 0.2 * (square * (theta[h] + conc))) + 0.025 * div
            lap = (c[h, e + 2, at, :] + c[h, e - 2, at, :]
                   + (c[h, e, pl.ds(r + 2, 8), :] + c[h, e, pl.ds(r - 2, 8), :]) + lz[h])
            store(h, old + step, conc + (0.025 * (lap - 6.0 * conc) + 0.5 * step))

    def flux_pair(p, start, gap, at_gap):
        def run(i, carry):
            e = start + 2 * i + jnp.where(i >= at_gap, gap, 0)
            flux(p, e)
            flux(p, e + 1)
            return carry
        return run

    def first_update(group):
        e0 = 4 * group + 2
        for r in ROWS:
            at = pl.ds(r, 8)
            low = [th[group, h, at, :] for h in range(2)]
            rise = [th[group + 1, h, at, :] - low[h] for h in range(2)]
            for q in range(4):
                theta = [low[h] + (0.125 + 0.25 * q) * rise[h] for h in range(2)]
                def store(h, new_p, new_c):
                    p1[h, e0 + q, at, :] = new_p
                    c1[h, e0 + q, at, :] = new_c
                update(p0, c0, e0 + q, r, theta, store)

    def second_update(group):
        e0 = 4 * group + 4
        for r in OWN:
            at = pl.ds(r, 8)
            to = pl.ds(r - RY, 8)
            total = [None, None]
            for q in range(4):
                low = [th[group + q // 2, h, at, :] for h in range(2)]
                rise = [th[group + q // 2 + 1, h, at, :] - low[h] for h in range(2)]
                frac = 0.125 + 0.25 * ((q + 2) % 4)
                theta = [low[h] + frac * rise[h] for h in range(2)]
                def store(h, new_p, new_c):
                    p2[h, e0 + q - M, to, :] = new_p
                    c2[h, e0 + q - M, to, :] = new_c
                    change = new_p - p0[h, e0 + q, at, :]
                    total[h] = change if total[h] is None else total[h] + change
                update(p1, c1, e0 + q, r, theta, store)
            for h in range(2):
                lat[group, to, pl.ds(h * LANES, LANES)] = total[h]

    for copy in y_copies:
        copy.wait_recv()
    lax.fori_loop(0, 7, flux_pair(p0, 5, 0, 99), 0)

    for copy in loads[5:]:
        copy.wait()
    for copy in h_copies:
        copy.wait_recv()
    coarse = [xr[0]] + [r1[pl.ds(x, 16, stride=8), :] for x in range(4)] + [xr[1]]
    on_rows = jnp.dot(jnp.concatenate(coarse, axis=0), wy[...], precision=HIGHEST, preferred_element_type=jnp.float32)
    for x in range(6):
        part = jnp.concatenate([on_rows[16 * x:16 * x + 16, LANES * z:LANES * z + LANES] for z in range(4)], axis=0)
        full = lax.dot_general(part, wz[...], (((0,), (0,)), ((), ())), precision=HIGHEST, preferred_element_type=jnp.float32)
        for h in range(2):
            th[x, h, pl.ds(4, 40), :] = full[:40, LANES * h:LANES * h + LANES]

    lax.fori_loop(1, 4, lambda i, carry: (first_update(i), carry)[1], 0)
    lax.fori_loop(0, 5, flux_pair(p1, 7, 0, 99), 0)
    lax.fori_loop(1, 3, lambda i, carry: (second_update(i), carry)[1], 0)

    def results(k, start, count):
        out = []
        for f, (src, dst) in enumerate(((p2, p_out), (c2, c_out))):
            for h in range(2):
                out.append(pltpu.make_async_copy(
                    src.at[h, pl.ds(start, count), :, :],
                    dst.at[pl.ds(start, count), :, pl.ds(h * LANES, LANES)],
                    out_sem.at[4 * k + 2 * f + h]))
        return out

    outs = results(0, 4, 8)
    for copy in outs:
        copy.start()

    for copy in x_copies + d_copies:
        copy.wait_recv()
    lax.fori_loop(0, 4, flux_pair(p0, 1, 14, 2), 0)
    lax.fori_loop(0, 2, lambda i, carry: (first_update(4 * i), carry)[1], 0)
    lax.fori_loop(0, 4, flux_pair(p1, 3, 10, 2), 0)
    lax.fori_loop(0, 2, lambda i, carry: (second_update(3 * i), carry)[1], 0)
    more = results(1, 0, 4) + results(2, 12, 4)
    for copy in more:
        copy.start()

    for x in range(4):
        on_y = jnp.dot(py[...], lat[x], precision=HIGHEST, preferred_element_type=jnp.float32)
        on_z = lax.dot_general(pz[...], on_y, (((1,), (1,)), ((), ())), precision=HIGHEST, preferred_element_type=jnp.float32)
        s2[pl.ds(x, 16, stride=8), :] = jnp.concatenate([on_z[16 * z:16 * z + 16] for z in range(4)], axis=1)
    l_copies = exchange(s2, r2, l_send, l_recv)
    for copy in l_copies:
        copy.start()
    r2[here, :] = s2[here, :]
    for copy in l_copies:
        copy.wait_recv()
    block = lane4 // 8
    for z in range(4):
        row = None
        for s in range(16):
            part = pltpu.roll(r2[pl.ds(8 * s, 4), :], (8 * s - 32 * z) % LANES, 1)
            row = part if row is None else jnp.where(block == s, part, row)
        lat_v[pl.ds(z, 4, stride=4), :] = row
    final = pltpu.make_async_copy(lat_v, lat_out, out_sem.at[12])
    final.start()

    for copy in x_copies + y_copies + d_copies + t_copies + h_copies + l_copies:
        copy.wait_send()
    for copy in outs + more:
        copy.wait()
    final.wait()


def body(nx, ny, phase, solute, macro_temp):
    macro = jnp.transpose(macro_temp, (0, 2, 1)).reshape(16, LANES)
    wy, wz, py, pz = (jnp.asarray(t) for t in tables(ny))
    f32 = jnp.float32
    anywhere = pl.BlockSpec(memory_space=pl.ANY)
    wide = pltpu.VMEM((2, EX, EY, LANES), f32)
    dma = pltpu.SemaphoreType.DMA
    new_phase, new_solute, latent = pl.pallas_call(
        functools.partial(kernel, nx, ny),
        out_shape=(jax.ShapeDtypeStruct(phase.shape, f32), jax.ShapeDtypeStruct(solute.shape, f32),
                   jax.ShapeDtypeStruct((16, LANES), f32)),
        in_specs=[anywhere] * 7,
        out_specs=(anywhere,) * 3,
        scratch_shapes=[wide] * 7 + [
            pltpu.VMEM((6, 2, EY, LANES), f32),
            pltpu.VMEM((2, BX, BY, LANES), f32), pltpu.VMEM((2, BX, BY, LANES), f32),
            pltpu.VMEM((4, BY, 2 * LANES), f32),
            pltpu.VMEM(wy.shape, f32), pltpu.VMEM(wz.shape, f32), pltpu.VMEM(py.shape, f32), pltpu.VMEM(pz.shape, f32),
            pltpu.VMEM((16, LANES), f32),
            pltpu.VMEM((128, LANES), f32), pltpu.VMEM((128, LANES), f32),
            pltpu.VMEM((2, 16, LANES), f32), pltpu.VMEM((2, 16, LANES), f32),
            pltpu.VMEM((128, LANES), f32), pltpu.VMEM((128, LANES), f32),
            pltpu.VMEM((16, LANES), f32),
            dma((9,)), dma((13,)), dma((4,)), dma((4,)), dma((4,)), dma((4,)), dma((8,)), dma((8,)),
            dma((16,)), dma((16,)), dma((2,)), dma((2,)), dma((16,)), dma((16,)),
        ],
        compiler_params=pltpu.CompilerParams(collective_id=0, has_side_effects=True, vmem_limit_bytes=40 << 20),
        name="substeps",
    )(phase, solute, macro, wy, wz, py, pz)
    return new_phase, new_solute, jnp.transpose(latent.reshape(4, 4, LANES), (0, 2, 1))


def solution(mesh):
    in_specs = (P("gx", "gy", None), P("gx", "gy", None), P("gx", None, "gy"))
    out_specs = (P("gx", "gy", None), P("gx", "gy", None), P("gx", None, "gy"))
    return jax.shard_map(
        functools.partial(body, mesh.shape["gx"], mesh.shape["gy"]),
        mesh=mesh, in_specs=in_specs, out_specs=out_specs, check_vma=False)
```

time: 127 us -> 47.4 us (0.37)
  starting transfers between devices: 50.8 us -> 0 us
  Pallas kernels: 0 us -> 38 us
  other arithmetic: 29.1 us -> 0 us
  local copies, waits for them, and re-layouts: 28.1 us -> 8.3 us
  waiting for transfers between devices: 16.7 us -> 0 us
  matrix products: 1.27 us -> 0 us
    pallas_call x0 -> x1, Pallas kernels: none -> 38 us  [body(): pl.pallas_call(functools.partial(kernel, nx, ny), out_shape=(jax.ShapeDty...]
    ppermute x12 -> x0, starting transfers between devices: 29.5 us -> none  [the longest x6 23.4 us: padded(): lax.ppermute(head, axis, [((i + 1) % count, i) for i in range(count)])]
    all_to_all x2 -> x0, starting transfers between devices: 21.3 us -> none  [the longest x1 12.9 us: body(): lax.all_to_all(restricted, 'gy', split_axis=2, concat_axis=1, tiled=True)]
    reshape x9 -> x0, local copies, waits for them, and re-layouts: 20.7 us -> none  [the longest x1 19.5 us: body(): change.reshape(cells_x // 4, 4, cells_y // 4, 4, cells_z // 4, 4)]
    ppermute x12 -> x0, waiting for transfers between devices: 13.3 us -> none  [the longest x6 9.15 us: padded(): lax.ppermute(tail, axis, [(i, (i + 1) % count) for i in range(count)])]
    mul x9 -> x0, other arithmetic: 11.9 us -> none  [the longest x2 3.45 us: divergence(): grad_x = 0.5 * (grid[2:, 1:-1, 1:-1] - grid[:-2, 1:-1, 1:-1])]
    reduce_sum x1 -> x0, other arithmetic: 7.1 us -> none  [body(): change.reshape(cells_x // 4, 4, cells_y // 4, 4, cells_z // 4, 4)]
    unnamed x11 -> x17, local copies, waits for them, and re-layouts: 3.06 us -> 8.3 us
  transfers between devices with their start and end apart: 14 -> 0, of which waited for: 9 -> 0; matrix products, arithmetic and copies ran while one was open for 7% -> 0% of each run, Pallas kernels for 0% -> 0%
where the time goes in v1:
time: 47.4 us; the launch traced here: 47 us
  Pallas kernels  38 us (80%)
  local copies, waits for them, and re-layouts  8.3 us (18%)
  between operations  0.65 us (1%)
    pallas_call x1, Pallas kernels, body(): pl.pallas_call(functools.partial(kernel, nx, ny), out_shape=(jax.ShapeDty...  38 us
    unnamed x17, local copies, waits for them, and re-layouts  8.3 us

profile of v1, /device:TPU:1, one launch (start us, length us, event | category | flops | bytes accessed | tf_op | source)
XLA Modules:
  0.0 47.0 jit_solution(3648572514120314397)
XLA Ops:
  0.6 0.0 copy-start
  0.6 1.0 %copy-done = f32[16,32,256]{2,1,0:T(8,128)S(1)} copy-done((f32[16,32,256]{2,1,0:T(8,128)S(1)}, f32[16,32,256]{2,1,0:T(8,128)}, u32[]{:S(2)}) %copy-start) | copy-done | bytes 524312
  1.7 0.0 copy-start.1
  1.7 1.0 %copy-done.1 = f32[16,32,256]{2,1,0:T(8,128)S(1)} copy-done((f32[16,32,256]{2,1,0:T(8,128)S(1)}, f32[16,32,256]{2,1,0:T(8,128)}, u32[]{:S(2)}) %copy-start.1) | copy-done | bytes 524312
  2.7 0.0 copy-start.2
  2.7 0.9 %copy-done.2 = f32[128,512]{1,0:T(8,128)S(1)} copy-done((f32[128,512]{1,0:T(8,128)S(1)}, f32[128,512]{1,0:T(8,128)}, u32[]{:S(2)}) %copy-start.2) | copy-done | bytes 262168
  3.7 0.0 copy-start.3
  3.7 0.8 %copy-done.3 = f32[64,256]{1,0:T(8,128)S(1)} copy-done((f32[64,256]{1,0:T(8,128)S(1)}, f32[64,256]{1,0:T(8,128)}, u32[]{:S(2)}) %copy-start.3) | copy-done | bytes 65560
  4.5 0.0 copy-start.4
  4.5 0.8 %copy-done.4 = f32[64,256]{1,0:T(8,128)S(1)} copy-done((f32[64,256]{1,0:T(8,128)S(1)}, f32[64,256]{1,0:T(8,128)}, u32[]{:S(2)}) %copy-start.4) | copy-done | bytes 65560
  5.3 0.0 copy-start.5
  5.3 0.7 %copy-done.5 = f32[32,32]{1,0:T(8,128)S(1)} copy-done((f32[32,32]{1,0:T(8,128)S(1)}, f32[32,32]{1,0:T(8,128)}, u32[]{:S(2)}) %copy-start.5) | copy-done | bytes 4120
  6.1 0.0 copy-start.6
  6.1 0.7 %copy-done.6 = f32[4,128,4]{1,2,0:T(4,128)S(1)} copy-done((f32[4,128,4]{1,2,0:T(4,128)S(1)}, f32[4,128,4]{1,2,0:T(4,128)}, u32[]{:S(2)}) %copy-start.6) | copy-done | bytes 8216
  6.8 38.0 %substeps.1 = (f32[16,32,256]{2,1,0:T(8,128)S(1)}, f32[16,32,256]{2,1,0:T(8,128)S(1)}, f32[16,128]{1,0:T(8,128)S(1)}) custom-call(f32[16,32,256]{2,1,0:T(8,128)S(1)} %copy-done, f32[16,32,256]{2,1,0:T(8,128)S(1)} %copy-done.1, f32[16,128]{1,0:T(8,128)S(1)} %bitcast.6, f32[128,512]{1,0:T(8,128)S(1)} %copy-done.2, f32[64,256]{1,0:T(8,128)S(1)} %copy-done.4, ...), custom_call_target="tpu_custom_call" | custom-call | tf_op jit(solution)/shard_map/substeps/pallas_call | solution.py:317
  44.8 0.8 %copy.13 = f32[16,32,256]{2,1,0:T(8,128)} copy(f32[16,32,256]{2,1,0:T(8,128)S(1)} %get-tuple-element.12) | data formatting | bytes 1048576
  45.6 0.8 %copy.14 = f32[16,32,256]{2,1,0:T(8,128)} copy(f32[16,32,256]{2,1,0:T(8,128)S(1)} %get-tuple-element.13) | data formatting | bytes 1048576
  46.4 0.6 %copy.15 = f32[4,128,4]{1,2,0:T(4,128)} copy(f32[4,128,4]{1,2,0:T(4,128)S(1)} %bitcast.7) | data formatting | bytes 16384
Async XLA Ops:
  0.6 1.0 %copy-start = (f32[16,32,256]{2,1,0:T(8,128)S(1)}, f32[16,32,256]{2,1,0:T(8,128)}, u32[]{:S(2)}) copy-start(f32[16,32,256]{2,1,0:T(8,128)} %p_in.1) | copy-start | bytes 1572868
  1.7 1.0 %copy-start.1 = (f32[16,32,256]{2,1,0:T(8,128)S(1)}, f32[16,32,256]{2,1,0:T(8,128)}, u32[]{:S(2)}) copy-start(f32[16,32,256]{2,1,0:T(8,128)} %c_in.1) | copy-start | bytes 1572868
  2.7 0.9 %copy-start.2 = (f32[128,512]{1,0:T(8,128)S(1)}, f32[128,512]{1,0:T(8,128)}, u32[]{:S(2)}) copy-start(f32[128,512]{1,0:T(8,128)} %constant.8.clone.wy_in) | copy-start | bytes 786436
  3.7 0.8 %copy-start.3 = (f32[64,256]{1,0:T(8,128)S(1)}, f32[64,256]{1,0:T(8,128)}, u32[]{:S(2)}) copy-start(f32[64,256]{1,0:T(8,128)} %constant.11.clone.pz_in) | copy-start | bytes 196612
  4.5 0.8 %copy-start.4 = (f32[64,256]{1,0:T(8,128)S(1)}, f32[64,256]{1,0:T(8,128)}, u32[]{:S(2)}) copy-start(f32[64,256]{1,0:T(8,128)} %constant.9.clone.wz_in) | copy-start | bytes 196612
  5.3 0.7 %copy-start.5 = (f32[32,32]{1,0:T(8,128)S(1)}, f32[32,32]{1,0:T(8,128)}, u32[]{:S(2)}) copy-start(f32[32,32]{1,0:T(8,128)} %constant.10.clone.py_in) | copy-start | bytes 12292
  6.1 0.7 %copy-start.6 = (f32[4,128,4]{1,2,0:T(4,128)S(1)}, f32[4,128,4]{1,2,0:T(4,128)}, u32[]{:S(2)}) copy-start(f32[4,128,4]{1,2,0:T(4,128)} %param.9) | copy-start | bytes 24580

commit v2 on v1

--- a/solution.py
+++ b/solution.py
@@ -311,7 +311,7 @@
     macro = jnp.transpose(macro_temp, (0, 2, 1)).reshape(16, LANES)
     wy, wz, py, pz = (jnp.asarray(t) for t in tables(ny))
     f32 = jnp.float32
-    anywhere = pl.BlockSpec(memory_space=pl.ANY)
+    anywhere = pl.BlockSpec(memory_space=pltpu.HBM)
     wide = pltpu.VMEM((2, EX, EY, LANES), f32)
     dma = pltpu.SemaphoreType.DMA
     new_phase, new_solute, latent = pl.pallas_call(
@@ -333,7 +333,7 @@
             dma((9,)), dma((13,)), dma((4,)), dma((4,)), dma((4,)), dma((4,)), dma((8,)), dma((8,)),
             dma((16,)), dma((16,)), dma((2,)), dma((2,)), dma((16,)), dma((16,)),
         ],
-        compiler_params=pltpu.CompilerParams(collective_id=0, has_side_effects=True, vmem_limit_bytes=40 << 20),
+        compiler_params=pltpu.CompilerParams(collective_id=0, has_side_effects=True, vmem_limit_bytes=60 << 20),
         name="substeps",
     )(phase, solute, macro, wy, wz, py, pz)
     return new_phase, new_solute, jnp.transpose(latent.reshape(4, 4, LANES), (0, 2, 1))

time: 47.4 us -> 42.4 us (0.89)
  local copies, waits for them, and re-layouts: 8.3 us -> 3.34 us
    unnamed x17 -> x7, local copies, waits for them, and re-layouts: 8.3 us -> 3.34 us
where the time goes in v2:
time: 42.4 us; the launch traced here: 42.3 us
  Pallas kernels  38.3 us (90%)
  local copies, waits for them, and re-layouts  3.34 us (8%)
  between operations  0.65 us (2%)
    pallas_call x1, Pallas kernels, body(): pl.pallas_call(functools.partial(kernel, nx, ny), out_shape=(jax.ShapeDty...  38.3 us
    unnamed x7, local copies, waits for them, and re-layouts  3.34 us

profile of v2, /device:TPU:1, one launch (start us, length us, event | category | flops | bytes accessed | tf_op | source)
XLA Modules:
  0.0 42.3 jit_solution(12507304525668807365)
XLA Ops:
  0.6 38.3 %substeps.1 = (f32[16,32,256]{2,1,0:T(8,128)}, f32[16,32,256]{2,1,0:T(8,128)}, f32[16,128]{1,0:T(8,128)}) custom-call(f32[16,32,256]{2,1,0:T(8,128)} %p_in.1, f32[16,32,256]{2,1,0:T(8,128)} %c_in.1, f32[16,128]{1,0:T(8,128)} %bitcast.6, f32[128,512]{1,0:T(8,128)} %constant.8.clone.wy_in, f32[64,256]{1,0:T(8,128)} %constant.9.clone.wz_in, ...), custom_call_target="tpu_custom_call" | custom-call | tf_op jit(solution)/shard_map/substeps/pallas_call | solution.py:317
  38.9 0.0 copy-start
  39.0 1.9 %copy.13 = f32[16,32,256]{2,1,0:T(8,128)} copy(f32[16,32,256]{2,1,0:T(8,128)} %get-tuple-element.12) | data formatting | bytes 1048576
  40.9 0.0 copy-done
  40.9 0.0 copy-start.1
  40.9 0.8 %copy.14 = f32[16,32,256]{2,1,0:T(8,128)} copy(f32[16,32,256]{2,1,0:T(8,128)S(1)} %copy-done) | data formatting | bytes 1048576
  41.7 0.0 copy-done.1
  41.7 0.6 %copy.15 = f32[4,128,4]{1,2,0:T(4,128)} copy(f32[4,128,4]{1,2,0:T(4,128)S(1)} %bitcast.7) | data formatting | bytes 16384
Async XLA Ops:
  38.9 2.0 %copy-start = (f32[16,32,256]{2,1,0:T(8,128)S(1)}, f32[16,32,256]{2,1,0:T(8,128)}, u32[]{:S(2)}) copy-start(f32[16,32,256]{2,1,0:T(8,128)} %get-tuple-element.13) | copy-start | bytes 1572868
  40.9 0.8 %copy-start.1 = (f32[16,128]{1,0:T(8,128)S(1)}, f32[16,128]{1,0:T(8,128)}, u32[]{:S(2)}) copy-start(f32[16,128]{1,0:T(8,128)} %get-tuple-element.8) | copy-start | bytes 24580

commit v3 on v2

v3 whole, which is shorter than its diff:
```python
import functools

import jax
import jax.numpy as jnp
import numpy as np
from jax import lax
from jax.experimental import pallas as pl
from jax.experimental.pallas import tpu as pltpu
from jax.sharding import PartitionSpec as P

MESH = pl.DeviceIdType.MESH

BX, BY = 16, 32
M = 4
EX = BX + 2 * M
RY = 8
EY = 48
LANES = 128
ROOT = 0.025 ** 0.5
ROWS = (4, 12, 20, 28, 36)
OWN = (8, 16, 24, 32)


def tables():
    wy = np.zeros((128, 4 * LANES), np.float32)
    for row in range(40):
        y = row - 4
        low = (2 * y - 3) // 8
        frac = (2 * y - 3 - 8 * low) / 8.0
        for hit, weight in ((low + 1, 1.0 - frac), (low + 2, frac)):
            if 0 <= hit < 10:
                for z in range(4):
                    wy[32 * z + hit, LANES * z + row] += weight
    wz = np.zeros((64, 256), np.float32)
    for fine in range(256):
        low = (2 * fine - 3) // 8
        frac = (2 * fine - 3 - 8 * low) / 8.0
        for hit, weight in ((low, 1.0 - frac), (low + 1, frac)):
            hit = min(max(hit, 0), 63)
            wz[16 * (hit % 4) + hit // 4, fine] += weight
    py = np.zeros((32, 128), np.float32)
    for row in range(128):
        py[row // 4, row] = 1.0
    pz = np.zeros((64, 256), np.float32)
    for fine in range(256):
        z = fine // 4
        pz[16 * (z % 4) + z // 4, fine] = 1.0 / 128.0
    tall = [np.concatenate([t] * 3, axis=0) for t in (wy, wz)]
    wide = [np.concatenate([t] * 3, axis=1) for t in (py, pz)]
    return [jnp.asarray(t, jnp.bfloat16) for t in tall + wide]


def three(value, axis):
    high = value.astype(jnp.bfloat16)
    rest = value - high.astype(jnp.float32)
    middle = rest.astype(jnp.bfloat16)
    low = (rest - middle.astype(jnp.float32)).astype(jnp.bfloat16)
    return jnp.concatenate([high, middle, low], axis=axis)


def kernel(nx, ny, p_in, c_in, m_in, wy_in, wz_in, py_in, pz_in, out, lat_v,
           pc0, pc1, fx, fy, fz, th, lat, wy, wz, py, pz, mac, s1, r1, xs, xr, s2, r2,
           load_sem, x_send, x_recv, y_send, y_recv, d_send, d_recv, t_send, t_recv, h_send, h_recv, l_send, l_recv):
    a = lax.axis_index("gx")
    b = lax.axis_index("gy")
    up_x, down_x = lax.rem(a + 1, nx), lax.rem(a + nx - 1, nx)
    up_y, down_y = lax.rem(b + 1, ny), lax.rem(b + ny - 1, ny)

    loads = []
    for f, src in enumerate((p_in, c_in)):
        for h in range(2):
            loads.append(pltpu.make_async_copy(
                src.at[:, :, pl.ds(h * LANES, LANES)],
                pc0.at[f, h, pl.ds(M, BX), pl.ds(RY, BY), :],
                load_sem.at[2 * f + h]))
    for k, (src, dst) in enumerate(((m_in, mac), (wy_in, wy), (wz_in, wz), (py_in, py), (pz_in, pz))):
        loads.append(pltpu.make_async_copy(src, dst, load_sem.at[4 + k]))
    loads[4].start()
    for copy in loads[:4] + loads[5:]:
        copy.start()

    barrier = pltpu.get_barrier_semaphore()
    corners = ((up_x, up_y), (up_x, down_y), (down_x, up_y), (down_x, down_y))
    peers = [(up_x, b), (down_x, b)] + list(corners)
    for k in range(1, ny):
        peers.append((a, lax.rem(b + k, ny)))
    for peer in peers:
        pl.semaphore_signal(barrier, inc=1, device_id=peer, device_id_type=MESH)

    lane = lax.broadcasted_iota(jnp.int32, (8, LANES), 1)
    first, last = lane == 0, lane == LANES - 1
    first2, last2 = lane < 2, lane >= LANES - 2

    loads[4].wait()
    lane4 = lax.broadcasted_iota(jnp.int32, (4, LANES), 1)
    zone = lane4 // 32
    layers = [mac[pl.ds(z, 4, stride=4), :] for z in range(4)]
    for dest in range(16):
        parts = [pltpu.roll(layers[z], (32 * z - 8 * dest + 1) % LANES, 1) for z in range(4)]
        tile = jnp.where(zone == 0, parts[0], jnp.where(zone == 1, parts[1], jnp.where(zone == 2, parts[2], parts[3])))
        s1[pl.ds(8 * dest, 4), :] = tile

    for copy in loads[:4]:
        copy.wait()
    pl.semaphore_wait(barrier, len(peers))

    x_copies, y_copies, d_copies = [], [], []
    lo, hi = pl.ds(M, M), pl.ds(BX, M)
    before, after = pl.ds(0, M), pl.ds(M + BX, M)
    row_lo, row_hi = pl.ds(RY, M), pl.ds(RY + BY - M, M)
    row_before, row_after = pl.ds(RY - M, M), pl.ds(RY + BY, M)
    rows, planes = pl.ds(RY, BY), pl.ds(M, BX)

    def remote(src, dst, send, recv, peer):
        return pltpu.make_async_remote_copy(
            src_ref=src, dst_ref=dst, send_sem=send, recv_sem=recv, device_id=peer, device_id_type=MESH)

    for k, (src, dst, peer) in enumerate(((hi, before, (up_x, b)), (lo, after, (down_x, b)))):
        x_copies.append(remote(pc0.at[:, :, src, rows, :], pc0.at[:, :, dst, rows, :], x_send.at[k], x_recv.at[k], peer))
    for k, (src, dst, peer) in enumerate(((row_hi, row_before, (a, up_y)), (row_lo, row_after, (a, down_y)))):
        y_copies.append(remote(pc0.at[:, :, planes, src, :], pc0.at[:, :, planes, dst, :], y_send.at[k], y_recv.at[k], peer))
    for k, (sx, dx, sy, dy, peer) in enumerate((
        (hi, before, row_hi, row_before, corners[0]),
        (hi, before, row_lo, row_after, corners[1]),
        (lo, after, row_hi, row_before, corners[2]),
        (lo, after, row_lo, row_after, corners[3]),
    )):
        d_copies.append(remote(pc0.at[:, :, sx, sy, :], pc0.at[:, :, dx, dy, :], d_send.at[k], d_recv.at[k], peer))

    def exchange(src, dst, send, recv):
        far, near, core = b // 8, (b // 2) % 4, b % 2
        steps = [(df, dn, dc) for df in (1, 0) for dn in (2, 1, 3, 0) for dc in (0, 1)]
        steps.sort(key=lambda d: -(2 * d[0] + min(d[1], 4 - d[1])))
        out = []
        for k, (df, dn, dc) in enumerate(d for d in steps if any(d)):
            to = ((far + df) % 2) * 8 + ((near + dn) % 4) * 2 + (core + dc) % 2
            out.append(remote(
                src.at[pl.ds(pl.multiple_of(8 * to, 8), 8), :], dst.at[pl.ds(pl.multiple_of(8 * b, 8), 8), :],
                send.at[k], recv.at[k], (a, to)))
        return out

    here = pl.ds(pl.multiple_of(8 * b, 8), 8)
    t_copies = exchange(s1, r1, t_send, t_recv)
    for copy in t_copies + x_copies + y_copies + d_copies:
        copy.start()
    r1[here, :] = s1[here, :]
    for copy in t_copies:
        copy.wait_recv()
    xs[0] = r1[pl.ds(3, 16, stride=8), :]
    xs[1] = r1[pl.ds(0, 16, stride=8), :]
    h_copies = [remote(xs.at[0], xr.at[0], h_send.at[0], h_recv.at[0], (up_x, b)),
                remote(xs.at[1], xr.at[1], h_send.at[1], h_recv.at[1], (down_x, b))]
    for copy in h_copies:
        copy.start()

    def flux(p, e):
        for r in ROWS:
            at = pl.ds(r, 8)
            v = [p[0, h, e, at, :] for h in range(2)]
            fwd = [pltpu.roll(v[h], 1, 1) for h in range(2)]
            bwd = [pltpu.roll(v[h], LANES - 1, 1) for h in range(2)]
            gz = [jnp.where(last, bwd[1], bwd[0]) - jnp.where(first, v[0], fwd[0]),
                  jnp.where(last, v[1], bwd[1]) - jnp.where(first, fwd[0], fwd[1])]
            wz_ = []
            for h in range(2):
                gx = p[0, h, e + 1, at, :] - p[0, h, e - 1, at, :]
                gy = p[0, h, e, pl.ds(r + 1, 8), :] - p[0, h, e, pl.ds(r - 1, 8), :]
                sx, sy = gx * gx, gy * gy
                total = sx + sy
                planar = total + 4.0
                ratio = (total * total - 8.0 * (sx * sy)) / (planar * planar)
                factor = ROOT + (0.3 * ROOT) * ratio
                stiff = factor * factor
                fx[h, e, at, :] = stiff * gx
                fy[h, e, at, :] = stiff * gy
                wz_.append(stiff * gz[h])
            fwd = [pltpu.roll(w, 1, 1) for w in wz_]
            bwd = [pltpu.roll(w, LANES - 1, 1) for w in wz_]
            fz[0, e, at, :] = jnp.where(last, bwd[1], bwd[0]) - jnp.where(first, 0.0, fwd[0])
            fz[1, e, at, :] = jnp.where(last, 0.0, bwd[1]) - jnp.where(first, fwd[0], fwd[1])

    def update(p, c, e, r, theta, store):
        at = pl.ds(r, 8)
        v = [c[1, h, e, at, :] for h in range(2)]
        fwd = [pltpu.roll(v[h], 2, 1) for h in range(2)]
        bwd = [pltpu.roll(v[h], LANES - 2, 1) for h in range(2)]
        head = jnp.where(first, v[0], pltpu.roll(v[0], 1, 1))
        tail = jnp.where(last, v[1], pltpu.roll(v[1], LANES - 1, 1))
        lz = [jnp.where(last2, bwd[1], bwd[0]) + jnp.where(first2, head, fwd[0]),
              jnp.where(last2, tail, bwd[1]) + jnp.where(first2, fwd[0], fwd[1])]
        for h in range(2):
            div = (fx[h, e + 1, at, :] - fx[h, e - 1, at, :]
                   + (fy[h, e, pl.ds(r + 1, 8), :] - fy[h, e, pl.ds(r - 1, 8), :]) + fz[h, e, at, :])
            old = p[0, h, e, at, :]
            conc = v[h]
            square = 1.0 - old * old
            step = square * (0.1 * old - 0.2 * (square * (theta[h] + conc))) + div
            lap = (c[1, h, e + 2, at, :] + c[1, h, e - 2, at, :]
                   + (c[1, h, e, pl.ds(r + 2, 8), :] + c[1, h, e, pl.ds(r - 2, 8), :]) + lz[h])
            store(h, old + step, 0.85 * conc + (0.025 * lap + 0.5 * step))

    def flux_planes(p, start, gap, count):
        def run(i, carry):
            for q in range(count):
                flux(p, start + gap * i + q)
            return carry
        return run

    def first_update(group):
        e0 = 4 * group + 2
        for r in ROWS:
            at = pl.ds(r, 8)
            low = [th[group, h, at, :] for h in range(2)]
            rise = [th[group + 1, h, at, :] - low[h] for h in range(2)]
            for q in range(4):
                theta = [low[h] + (0.125 + 0.25 * q) * rise[h] for h in range(2)]
                def store(h, new_p, new_c):
                    pc1[0, h, e0 + q, at, :] = new_p
                    pc1[1, h, e0 + q, at, :] = new_c
                update(pc0, pc0, e0 + q, r, theta, store)

    def second_update(group):
        e0 = 4 * group + 4
        for r in OWN:
            at = pl.ds(r, 8)
            to = pl.ds(r - RY, 8)
            total = [None, None]
            for q in range(4):
                low = [th[group + q // 2, h, at, :] for h in range(2)]
                rise = [th[group + q // 2 + 1, h, at, :] - low[h] for h in range(2)]
                frac = 0.125 + 0.25 * ((q + 2) % 4)
                theta = [low[h] + frac * rise[h] for h in range(2)]
                def store(h, new_p, new_c):
                    out[0, h, e0 + q - M, to, :] = new_p
                    out[1, h, e0 + q - M, to, :] = new_c
                    change = new_p - pc0[0, h, e0 + q, at, :]
                    total[h] = change if total[h] is None else total[h] + change
                update(pc1, pc1, e0 + q, r, theta, store)
            for h in range(2):
                lat[pl.ds(pl.multiple_of(BY * group + r - RY, 8), 8), pl.ds(h * LANES, LANES)] = total[h]

    for copy in y_copies:
        copy.wait_recv()
    lax.fori_loop(0, 2, flux_planes(pc0, 5, 7, 7), 0)

    for copy in loads[5:]:
        copy.wait()

    def temperature(first_x, coarse):
        count = len(coarse)
        on_rows = jnp.dot(three(jnp.concatenate(coarse, axis=0), 1), wy[...], preferred_element_type=jnp.float32)
        parts = []
        for x in range(count):
            part = jnp.concatenate([on_rows[16 * x:16 * x + 16, LANES * z:LANES * z + LANES] for z in range(4)], axis=0)
            parts.append(jnp.transpose(part)[:40])
        full = jnp.dot(three(jnp.concatenate(parts, axis=0), 1), wz[...], preferred_element_type=jnp.float32)
        for x in range(count):
            for h in range(2):
                th[first_x[x], h, pl.ds(4, 40), :] = full[40 * x:40 * x + 40, LANES * h:LANES * h + LANES]

    temperature((1, 2, 3, 4), [r1[pl.ds(x, 16, stride=8), :] for x in range(4)])
    lax.fori_loop(1, 4, lambda i, carry: (first_update(i), carry)[1], 0)
    lax.fori_loop(0, 2, flux_planes(pc1, 7, 5, 5), 0)
    lax.fori_loop(1, 3, lambda i, carry: (second_update(i), carry)[1], 0)
    for copy in h_copies:
        copy.wait_recv()
    temperature((0, 5), [xr[0], xr[1]])

    for copy in x_copies + d_copies:
        copy.wait_recv()
    lax.fori_loop(0, 2, flux_planes(pc0, 1, 18, 4), 0)
    lax.fori_loop(0, 2, lambda i, carry: (first_update(4 * i), carry)[1], 0)
    lax.fori_loop(0, 2, flux_planes(pc1, 3, 14, 4), 0)
    lax.fori_loop(0, 2, lambda i, carry: (second_update(3 * i), carry)[1], 0)

    on_y = jnp.dot(py[...], three(lat[...], 0), preferred_element_type=jnp.float32)
    on_z = lax.dot_general(pz[...], three(on_y, 1), (((1,), (1,)), ((), ())), preferred_element_type=jnp.float32)
    for z in range(4):
        s2[pl.ds(z, 16, stride=8), pl.ds(0, 32)] = on_z[16 * z:16 * z + 16]
    l_copies = exchange(s2, r2, l_send, l_recv)
    for copy in l_copies:
        copy.start()
    r2[here, :] = s2[here, :]
    for copy in l_copies:
        copy.wait_recv()
    block = lane4 // 8
    for x in range(4):
        row = None
        for s in range(16):
            part = pltpu.roll(r2[pl.ds(8 * s, 4), :], (8 * s - 8 * x) % LANES, 1)
            row = part if row is None else jnp.where(block == s, part, row)
        lat_v[pl.ds(4 * x, 4), :] = row

    for copy in x_copies + y_copies + d_copies + t_copies + h_copies + l_copies:
        copy.wait_send()


def store_kernel(field, lat, p_out, c_out, lat_out, sem):
    copies = [pltpu.make_async_copy(lat, lat_out, sem.at[4])]
    for f, dst in enumerate((p_out, c_out)):
        for h in range(2):
            copies.append(pltpu.make_async_copy(field.at[f, h], dst.at[:, :, pl.ds(h * LANES, LANES)], sem.at[2 * f + h]))
    for copy in copies:
        copy.start()
    for copy in copies:
        copy.wait()


def body(nx, ny, phase, solute, macro_temp):
    macro = jnp.transpose(macro_temp, (0, 2, 1)).reshape(16, LANES)
    weights = tables()
    f32 = jnp.float32
    anywhere = pl.BlockSpec(memory_space=pl.ANY)
    here = pl.BlockSpec(memory_space=pltpu.VMEM)
    wide = pltpu.VMEM((2, EX, EY, LANES), f32)
    both = pltpu.VMEM((2, 2, EX, EY, LANES), f32)
    dma = pltpu.SemaphoreType.DMA
    field, latent = pl.pallas_call(
        functools.partial(kernel, nx, ny),
        out_shape=(pltpu.VMEM((2, 2, BX, BY, LANES), f32), pltpu.VMEM((16, LANES), f32)),
        in_specs=[anywhere] * 7,
        out_specs=(here, here),
        scratch_shapes=[both] * 2 + [wide] * 3 + [
            pltpu.VMEM((6, 2, EY, LANES), f32),
            pltpu.VMEM((4 * BY, 2 * LANES), f32)] + [
            pltpu.VMEM(w.shape, w.dtype) for w in weights] + [
            pltpu.VMEM((16, LANES), f32),
            pltpu.VMEM((128, LANES), f32), pltpu.VMEM((128, LANES), f32),
            pltpu.VMEM((2, 16, LANES), f32), pltpu.VMEM((2, 16, LANES), f32),
            pltpu.VMEM((128, LANES), f32), pltpu.VMEM((128, LANES), f32),
            dma((9,)), dma((2,)), dma((2,)), dma((2,)), dma((2,)), dma((4,)), dma((4,)),
            dma((16,)), dma((16,)), dma((2,)), dma((2,)), dma((16,)), dma((16,)),
        ],
        compiler_params=pltpu.CompilerParams(collective_id=0, has_side_effects=True, vmem_limit_bytes=60 << 20),
        name="substeps",
    )(phase, solute, macro, *weights)
    new_phase, new_solute, latent = pl.pallas_call(
        store_kernel,
        out_shape=(jax.ShapeDtypeStruct(phase.shape, f32), jax.ShapeDtypeStruct(solute.shape, f32),
                   jax.ShapeDtypeStruct((16, LANES), f32)),
        in_specs=[anywhere] * 2,
        out_specs=(anywhere,) * 3,
        scratch_shapes=[dma((5,))],
        compiler_params=pltpu.CompilerParams(vmem_limit_bytes=1 << 20),
        name="store",
    )(field, latent)
    return new_phase, new_solute, jnp.transpose(latent.reshape(4, 4, LANES), (0, 2, 1))


def solution(mesh):
    in_specs = (P("gx", "gy", None), P("gx", "gy", None), P("gx", None, "gy"))
    out_specs = (P("gx", "gy", None), P("gx", "gy", None), P("gx", None, "gy"))
    return jax.shard_map(
        functools.partial(body, mesh.shape["gx"], mesh.shape["gy"]),
        mesh=mesh, in_specs=in_specs, out_specs=out_specs, check_vma=False)
```

time: 42.4 us -> 36.3 us (0.86)
  local copies, waits for them, and re-layouts: 3.34 us -> 0 us
  Pallas kernels: 38.3 us -> 35.6 us
    unnamed x7 -> x0, local copies, waits for them, and re-layouts: 3.34 us -> none
    pallas_call x1 -> x2, Pallas kernels: 38.3 us -> 35.6 us  [the longest x1 34.6 us: body(): pl.pallas_call(functools.partial(kernel, nx, ny), out_shape=(pltpu.VMEM((...]
where the time goes in v3:
time: 36.3 us; the launch traced here: 36.2 us
  Pallas kernels  35.6 us (98%)
  between operations  0.64 us (2%)
    pallas_call x1, Pallas kernels, body(): pl.pallas_call(functools.partial(kernel, nx, ny), out_shape=(pltpu.VMEM((...  34.6 us
    pallas_call x1, Pallas kernels, body(): pl.pallas_call(store_kernel, out_shape=(jax.ShapeDtypeStruct(phase.shape,...  1.01 us

profile of v3, /device:TPU:1, one launch (start us, length us, event | category | flops | bytes accessed | tf_op | source)
XLA Modules:
  0.0 36.2 jit_solution(16401870151852379963)
XLA Ops:
  0.6 34.6 %substeps.1 = (f32[2,2,16,32,128]{4,3,2,1,0:T(8,128)S(1)}, f32[16,128]{1,0:T(8,128)S(1)}) custom-call(f32[16,32,256]{2,1,0:T(8,128)} %p_in.1, f32[16,32,256]{2,1,0:T(8,128)} %c_in.1, f32[16,128]{1,0:T(8,128)} %bitcast.6, bf16[384,512]{1,0:T(8,128)(2,1)} %constant.8.clone.wy_in, bf16[192,256]{1,0:T(8,128)(2,1)} %constant.9.clone.wz_in, ...), custom_call_target="tpu_custom_call" | custom-call | tf_op jit(solution)/shard_map/substeps/pallas_call | solution.py:318
  35.2 1.0 %store.1 = (f32[16,32,256]{2,1,0:T(8,128)}, f32[16,32,256]{2,1,0:T(8,128)}, f32[16,128]{1,0:T(8,128)}) custom-call(f32[2,2,16,32,128]{4,3,2,1,0:T(8,128)S(1)} %get-tuple-element.8.field, f32[16,128]{1,0:T(8,128)S(1)} %get-tuple-element.9.lat), custom_call_target="tpu_custom_call" | custom-call | tf_op jit(solution)/shard_map/store/pallas_call | solution.py:337

commit v4 on v3

--- a/solution.py
+++ b/solution.py
@@ -119,11 +119,13 @@
         x_copies.append(remote(pc0.at[:, :, src, rows, :], pc0.at[:, :, dst, rows, :], x_send.at[k], x_recv.at[k], peer))
     for k, (src, dst, peer) in enumerate(((row_hi, row_before, (a, up_y)), (row_lo, row_after, (a, down_y)))):
         y_copies.append(remote(pc0.at[:, :, planes, src, :], pc0.at[:, :, planes, dst, :], y_send.at[k], y_recv.at[k], peer))
+    first3, last3, before3, after3 = pl.ds(M, 3), pl.ds(BX + 1, 3), pl.ds(1, 3), pl.ds(M + BX, 3)
+    rows_lo, rows_hi, rows_before, rows_after = pl.ds(RY, 3), pl.ds(RY + BY - 3, 3), pl.ds(RY - 3, 3), pl.ds(RY + BY, 3)
     for k, (sx, dx, sy, dy, peer) in enumerate((
-        (hi, before, row_hi, row_before, corners[0]),
-        (hi, before, row_lo, row_after, corners[1]),
-        (lo, after, row_hi, row_before, corners[2]),
-        (lo, after, row_lo, row_after, corners[3]),
+        (last3, before3, rows_hi, rows_before, corners[0]),
+        (last3, before3, rows_lo, rows_after, corners[1]),
+        (first3, after3, rows_hi, rows_before, corners[2]),
+        (first3, after3, rows_lo, rows_after, corners[3]),
     )):
         d_copies.append(remote(pc0.at[:, :, sx, sy, :], pc0.at[:, :, dx, dy, :], d_send.at[k], d_recv.at[k], peer))
 
@@ -141,27 +143,18 @@
 
     here = pl.ds(pl.multiple_of(8 * b, 8), 8)
     t_copies = exchange(s1, r1, t_send, t_recv)
-    for copy in t_copies + x_copies + y_copies + d_copies:
+    for copy in d_copies + t_copies + y_copies + x_copies:
         copy.start()
     r1[here, :] = s1[here, :]
-    for copy in t_copies:
-        copy.wait_recv()
-    xs[0] = r1[pl.ds(3, 16, stride=8), :]
-    xs[1] = r1[pl.ds(0, 16, stride=8), :]
-    h_copies = [remote(xs.at[0], xr.at[0], h_send.at[0], h_recv.at[0], (up_x, b)),
-                remote(xs.at[1], xr.at[1], h_send.at[1], h_recv.at[1], (down_x, b))]
-    for copy in h_copies:
-        copy.start()
-
-    def flux(p, e):
-        for r in ROWS:
-            at = pl.ds(r, 8)
+    def flux(p, planes_):
+        tiles = [(e, pl.ds(r, 8), r) for e in planes_ for r in ROWS]
+        for e, at, r in tiles:
             v = [p[0, h, e, at, :] for h in range(2)]
             fwd = [pltpu.roll(v[h], 1, 1) for h in range(2)]
             bwd = [pltpu.roll(v[h], LANES - 1, 1) for h in range(2)]
-            gz = [jnp.where(last, bwd[1], bwd[0]) - jnp.where(first, v[0], fwd[0]),
-                  jnp.where(last, v[1], bwd[1]) - jnp.where(first, fwd[0], fwd[1])]
-            wz_ = []
+            fz[0, e, at, :] = jnp.where(last, bwd[1], bwd[0]) - jnp.where(first, v[0], fwd[0])
+            fz[1, e, at, :] = jnp.where(last, v[1], bwd[1]) - jnp.where(first, fwd[0], fwd[1])
+        for e, at, r in tiles:
             for h in range(2):
                 gx = p[0, h, e + 1, at, :] - p[0, h, e - 1, at, :]
                 gy = p[0, h, e, pl.ds(r + 1, 8), :] - p[0, h, e, pl.ds(r - 1, 8), :]
@@ -173,36 +166,42 @@
                 stiff = factor * factor
                 fx[h, e, at, :] = stiff * gx
                 fy[h, e, at, :] = stiff * gy
-                wz_.append(stiff * gz[h])
-            fwd = [pltpu.roll(w, 1, 1) for w in wz_]
-            bwd = [pltpu.roll(w, LANES - 1, 1) for w in wz_]
+                fz[h, e, at, :] = stiff * fz[h, e, at, :]
+        for e, at, r in tiles:
+            w = [fz[h, e, at, :] for h in range(2)]
+            fwd = [pltpu.roll(w[h], 1, 1) for h in range(2)]
+            bwd = [pltpu.roll(w[h], LANES - 1, 1) for h in range(2)]
             fz[0, e, at, :] = jnp.where(last, bwd[1], bwd[0]) - jnp.where(first, 0.0, fwd[0])
             fz[1, e, at, :] = jnp.where(last, 0.0, bwd[1]) - jnp.where(first, fwd[0], fwd[1])
 
-    def update(p, c, e, r, theta, store):
+    def new_phase(pc, h, e, r, theta):
         at = pl.ds(r, 8)
-        v = [c[1, h, e, at, :] for h in range(2)]
+        div = (fx[h, e + 1, at, :] - fx[h, e - 1, at, :]
+               + (fy[h, e, pl.ds(r + 1, 8), :] - fy[h, e, pl.ds(r - 1, 8), :]) + fz[h, e, at, :])
+        old, conc = pc[0, h, e, at, :], pc[1, h, e, at, :]
+        square = 1.0 - old * old
+        step = square * (0.1 * old - 0.2 * (square * (theta + conc))) + div
+        return old + step, step
+
+    def new_solute(pc, e, r, steps):
+        at = pl.ds(r, 8)
+        v = [pc[1, h, e, at, :] for h in range(2)]
         fwd = [pltpu.roll(v[h], 2, 1) for h in range(2)]
         bwd = [pltpu.roll(v[h], LANES - 2, 1) for h in range(2)]
         head = jnp.where(first, v[0], pltpu.roll(v[0], 1, 1))
         tail = jnp.where(last, v[1], pltpu.roll(v[1], LANES - 1, 1))
         lz = [jnp.where(last2, bwd[1], bwd[0]) + jnp.where(first2, head, fwd[0]),
               jnp.where(last2, tail, bwd[1]) + jnp.where(first2, fwd[0], fwd[1])]
+        out = []
         for h in range(2):
-            div = (fx[h, e + 1, at, :] - fx[h, e - 1, at, :]
-                   + (fy[h, e, pl.ds(r + 1, 8), :] - fy[h, e, pl.ds(r - 1, 8), :]) + fz[h, e, at, :])
-            old = p[0, h, e, at, :]
-            conc = v[h]
-            square = 1.0 - old * old
-            step = square * (0.1 * old - 0.2 * (square * (theta[h] + conc))) + div
-            lap = (c[1, h, e + 2, at, :] + c[1, h, e - 2, at, :]
-                   + (c[1, h, e, pl.ds(r + 2, 8), :] + c[1, h, e, pl.ds(r - 2, 8), :]) + lz[h])
-            store(h, old + step, 0.85 * conc + (0.025 * lap + 0.5 * step))
+            lap = (pc[1, h, e + 2, at, :] + pc[1, h, e - 2, at, :]
+                   + (pc[1, h, e, pl.ds(r + 2, 8), :] + pc[1, h, e, pl.ds(r - 2, 8), :]) + lz[h])
+            out.append(0.85 * v[h] + (0.025 * lap + 0.5 * steps[h]))
+        return out
 
     def flux_planes(p, start, gap, count):
         def run(i, carry):
-            for q in range(count):
-                flux(p, start + gap * i + q)
+            flux(p, [start + gap * i + q for q in range(count)])
             return carry
         return run
 
@@ -213,35 +212,57 @@
             low = [th[group, h, at, :] for h in range(2)]
             rise = [th[group + 1, h, at, :] - low[h] for h in range(2)]
             for q in range(4):
-                theta = [low[h] + (0.125 + 0.25 * q) * rise[h] for h in range(2)]
-                def store(h, new_p, new_c):
-                    pc1[0, h, e0 + q, at, :] = new_p
-                    pc1[1, h, e0 + q, at, :] = new_c
-                update(pc0, pc0, e0 + q, r, theta, store)
-
-    def second_update(group):
+                steps = []
+                for h in range(2):
+                    new, step = new_phase(pc0, h, e0 + q, r, low[h] + (0.125 + 0.25 * q) * rise[h])
+                    pc1[0, h, e0 + q, at, :] = new
+                    steps.append(step)
+                for h, new in enumerate(new_solute(pc0, e0 + q, r, steps)):
+                    pc1[1, h, e0 + q, at, :] = new
+
+    def second_update(group, with_solute):
         e0 = 4 * group + 4
         for r in OWN:
             at = pl.ds(r, 8)
             to = pl.ds(r - RY, 8)
             total = [None, None]
             for q in range(4):
-                low = [th[group + q // 2, h, at, :] for h in range(2)]
-                rise = [th[group + q // 2 + 1, h, at, :] - low[h] for h in range(2)]
                 frac = 0.125 + 0.25 * ((q + 2) % 4)
-                theta = [low[h] + frac * rise[h] for h in range(2)]
-                def store(h, new_p, new_c):
-                    out[0, h, e0 + q - M, to, :] = new_p
-                    out[1, h, e0 + q - M, to, :] = new_c
-                    change = new_p - pc0[0, h, e0 + q, at, :]
+                steps = []
+                for h in range(2):
+                    low = th[group + q // 2, h, at, :]
+                    new, step = new_phase(pc1, h, e0 + q, r, low + frac * (th[group + q // 2 + 1, h, at, :] - low))
+                    out[0, h, e0 + q - M, to, :] = new
+                    change = new - pc0[0, h, e0 + q, at, :]
                     total[h] = change if total[h] is None else total[h] + change
-                update(pc1, pc1, e0 + q, r, theta, store)
+                    steps.append(step)
+                if with_solute:
+                    for h, new in enumerate(new_solute(pc1, e0 + q, r, steps)):
+                        out[1, h, e0 + q - M, to, :] = new
             for h in range(2):
                 lat[pl.ds(pl.multiple_of(BY * group + r - RY, 8), 8), pl.ds(h * LANES, LANES)] = total[h]
+
+    def late_solute(group):
+        e0 = 4 * group + 4
+        for r in OWN:
+            to = pl.ds(r - RY, 8)
+            for q in range(4):
+                steps = [out[0, h, e0 + q - M, to, :] - pc1[0, h, e0 + q, pl.ds(r, 8), :] for h in range(2)]
+                for h, new in enumerate(new_solute(pc1, e0 + q, r, steps)):
+                    out[1, h, e0 + q - M, to, :] = new
 
     for copy in y_copies:
         copy.wait_recv()
     lax.fori_loop(0, 2, flux_planes(pc0, 5, 7, 7), 0)
+    for copy in t_copies:
+        copy.wait_recv()
+    xs[0] = r1[pl.ds(3, 16, stride=8), :]
+    xs[1] = r1[pl.ds(0, 16, stride=8), :]
+    h_copies = [remote(xs.at[0], xr.at[0], h_send.at[0], h_recv.at[0], (up_x, b)),
+                remote(xs.at[1], xr.at[1], h_send.at[1], h_recv.at[1], (down_x, b))]
+    for copy in h_copies:
+        copy.start()
+
 
     for copy in loads[5:]:
         copy.wait()
@@ -261,17 +282,17 @@
     temperature((1, 2, 3, 4), [r1[pl.ds(x, 16, stride=8), :] for x in range(4)])
     lax.fori_loop(1, 4, lambda i, carry: (first_update(i), carry)[1], 0)
     lax.fori_loop(0, 2, flux_planes(pc1, 7, 5, 5), 0)
-    lax.fori_loop(1, 3, lambda i, carry: (second_update(i), carry)[1], 0)
-    for copy in h_copies:
-        copy.wait_recv()
-    temperature((0, 5), [xr[0], xr[1]])
-
-    for copy in x_copies + d_copies:
-        copy.wait_recv()
-    lax.fori_loop(0, 2, flux_planes(pc0, 1, 18, 4), 0)
-    lax.fori_loop(0, 2, lambda i, carry: (first_update(4 * i), carry)[1], 0)
-    lax.fori_loop(0, 2, flux_planes(pc1, 3, 14, 4), 0)
-    lax.fori_loop(0, 2, lambda i, carry: (second_update(3 * i), carry)[1], 0)
+    lax.fori_loop(1, 3, lambda i, carry: (second_update(i, True), carry)[1], 0)
+
+    for side in (1, 0):
+        for copy in [x_copies[side]] + d_copies[2 * side:2 * side + 2]:
+            copy.wait_recv()
+        flux(pc0, [(1, 19)[side] + q for q in range(4)])
+        h_copies[side].wait_recv()
+        temperature(((0,), (5,))[side], [xr[side]])
+        first_update((0, 4)[side])
+        flux(pc1, [(3, 17)[side] + q for q in range(4)])
+        second_update((0, 3)[side], False)
 
     on_y = jnp.dot(py[...], three(lat[...], 0), preferred_element_type=jnp.float32)
     on_z = lax.dot_general(pz[...], three(on_y, 1), (((1,), (1,)), ((), ())), preferred_element_type=jnp.float32)
@@ -281,6 +302,7 @@
     for copy in l_copies:
         copy.start()
     r2[here, :] = s2[here, :]
+    lax.fori_loop(0, 2, lambda i, carry: (late_solute(3 * i), carry)[1], 0)
     for copy in l_copies:
         copy.wait_recv()
     block = lane4 // 8

time: 36.3 us -> 32.7 us (0.901)
  Pallas kernels: 35.6 us -> 32 us
    pallas_call x1, Pallas kernels: 34.6 us -> 31 us  [body(): pl.pallas_call(functools.partial(kernel, nx, ny), out_shape=(pltpu.VMEM((...]
where the time goes in v4:
time: 32.7 us; the launch traced here: 32.6 us
  Pallas kernels  32 us (98%)
  between operations  0.64 us (2%)
    pallas_call x1, Pallas kernels, body(): pl.pallas_call(functools.partial(kernel, nx, ny), out_shape=(pltpu.VMEM((...  31 us
    pallas_call x1, Pallas kernels, body(): pl.pallas_call(store_kernel, out_shape=(jax.ShapeDtypeStruct(phase.shape,...  1.01 us

profile of v4, /device:TPU:1, one launch (start us, length us, event | category | flops | bytes accessed | tf_op | source)
XLA Modules:
  0.0 32.6 jit_solution(5685479648245918489)
XLA Ops:
  0.6 31.0 %substeps.1 = (f32[2,2,16,32,128]{4,3,2,1,0:T(8,128)S(1)}, f32[16,128]{1,0:T(8,128)S(1)}) custom-call(f32[16,32,256]{2,1,0:T(8,128)} %p_in.1, f32[16,32,256]{2,1,0:T(8,128)} %c_in.1, f32[16,128]{1,0:T(8,128)} %bitcast.6, bf16[384,512]{1,0:T(8,128)(2,1)} %constant.8.clone.wy_in, bf16[192,256]{1,0:T(8,128)(2,1)} %constant.9.clone.wz_in, ...), custom_call_target="tpu_custom_call" | custom-call | tf_op jit(solution)/shard_map/substeps/pallas_call | solution.py:340
  31.6 1.0 %store.1 = (f32[16,32,256]{2,1,0:T(8,128)}, f32[16,32,256]{2,1,0:T(8,128)}, f32[16,128]{1,0:T(8,128)}) custom-call(f32[2,2,16,32,128]{4,3,2,1,0:T(8,128)S(1)} %get-tuple-element.8.field, f32[16,128]{1,0:T(8,128)S(1)} %get-tuple-element.9.lat), custom_call_target="tpu_custom_call" | custom-call | tf_op jit(solution)/shard_map/store/pallas_call | solution.py:359

commit v5 on v4

--- a/solution.py
+++ b/solution.py
@@ -137,13 +137,13 @@
         for k, (df, dn, dc) in enumerate(d for d in steps if any(d)):
             to = ((far + df) % 2) * 8 + ((near + dn) % 4) * 2 + (core + dc) % 2
             out.append(remote(
-                src.at[pl.ds(pl.multiple_of(8 * to, 8), 8), :], dst.at[pl.ds(pl.multiple_of(8 * b, 8), 8), :],
+                src.at[pl.ds(pl.multiple_of(8 * to, 8), 4), :], dst.at[pl.ds(pl.multiple_of(8 * b, 8), 4), :],
                 send.at[k], recv.at[k], (a, to)))
         return out
 
-    here = pl.ds(pl.multiple_of(8 * b, 8), 8)
+    here = pl.ds(pl.multiple_of(8 * b, 8), 4)
     t_copies = exchange(s1, r1, t_send, t_recv)
-    for copy in d_copies + t_copies + y_copies + x_copies:
+    for copy in t_copies + d_copies + x_copies + y_copies:
         copy.start()
     r1[here, :] = s1[here, :]
     def flux(p, planes_):

time: 32.7 us -> 30.7 us (0.939)
  Pallas kernels: 32 us -> 29.9 us
    pallas_call x1, Pallas kernels: 31 us -> 28.9 us  [body(): pl.pallas_call(functools.partial(kernel, nx, ny), out_shape=(pltpu.VMEM((...]
where the time goes in v5:
time: 30.7 us; the launch traced here: 30.6 us
  Pallas kernels  29.9 us (97%)
  between operations  0.64 us (2%)
    pallas_call x1, Pallas kernels, body(): pl.pallas_call(functools.partial(kernel, nx, ny), out_shape=(pltpu.VMEM((...  28.9 us
    pallas_call x1, Pallas kernels, body(): pl.pallas_call(store_kernel, out_shape=(jax.ShapeDtypeStruct(phase.shape,...  1.01 us

profile of v5, /device:TPU:1, one launch (start us, length us, event | category | flops | bytes accessed | tf_op | source)
XLA Modules:
  0.0 30.6 jit_solution(14570651472190967554)
XLA Ops:
  0.6 28.9 %substeps.1 = (f32[2,2,16,32,128]{4,3,2,1,0:T(8,128)S(1)}, f32[16,128]{1,0:T(8,128)S(1)}) custom-call(f32[16,32,256]{2,1,0:T(8,128)} %p_in.1, f32[16,32,256]{2,1,0:T(8,128)} %c_in.1, f32[16,128]{1,0:T(8,128)} %bitcast.6, bf16[384,512]{1,0:T(8,128)(2,1)} %constant.8.clone.wy_in, bf16[192,256]{1,0:T(8,128)(2,1)} %constant.9.clone.wz_in, ...), custom_call_target="tpu_custom_call" | custom-call | tf_op jit(solution)/shard_map/substeps/pallas_call | solution.py:340
  29.6 1.0 %store.1 = (f32[16,32,256]{2,1,0:T(8,128)}, f32[16,32,256]{2,1,0:T(8,128)}, f32[16,128]{1,0:T(8,128)}) custom-call(f32[2,2,16,32,128]{4,3,2,1,0:T(8,128)S(1)} %get-tuple-element.8.field, f32[16,128]{1,0:T(8,128)S(1)} %get-tuple-element.9.lat), custom_call_target="tpu_custom_call" | custom-call | tf_op jit(solution)/shard_map/store/pallas_call | solution.py:359

commit v6 on v5

--- a/solution.py
+++ b/solution.py
@@ -38,8 +38,8 @@
         for hit, weight in ((low, 1.0 - frac), (low + 1, frac)):
             hit = min(max(hit, 0), 63)
             wz[16 * (hit % 4) + hit // 4, fine] += weight
-    py = np.zeros((32, 128), np.float32)
-    for row in range(128):
+    py = np.zeros((16, BY), np.float32)
+    for row in range(BY):
         py[row // 4, row] = 1.0
     pz = np.zeros((64, 256), np.float32)
     for fine in range(256):
@@ -59,12 +59,22 @@
 
 
 def kernel(nx, ny, p_in, c_in, m_in, wy_in, wz_in, py_in, pz_in, out, lat_v,
-           pc0, pc1, fx, fy, fz, th, lat, wy, wz, py, pz, mac, s1, r1, xs, xr, s2, r2,
+           pc0, pc1, fx, fy, fz, th, lat, oy, wy, wz, py, pz, mac, s1, r1, xs, xr, s2, r2,
            load_sem, x_send, x_recv, y_send, y_recv, d_send, d_recv, t_send, t_recv, h_send, h_recv, l_send, l_recv):
     a = lax.axis_index("gx")
     b = lax.axis_index("gy")
     up_x, down_x = lax.rem(a + 1, nx), lax.rem(a + nx - 1, nx)
     up_y, down_y = lax.rem(b + 1, ny), lax.rem(b + ny - 1, ny)
+
+    barrier = pltpu.get_barrier_semaphore()
+    corners = ((up_x, up_y), (up_x, down_y), (down_x, up_y), (down_x, down_y))
+    far, near, core = b // 8, (b // 2) % 4, b % 2
+    steps = [(df, dn, dc) for df in (1, 0) for dn in (2, 1, 3, 0) for dc in (0, 1)][:-2] + [(0, 0, 1)]
+    steps.sort(key=lambda d: -(2 * d[0] + min(d[1], 4 - d[1])))
+    others = [((far + df) % 2) * 8 + ((near + dn) % 4) * 2 + (core + dc) % 2 for df, dn, dc in steps]
+    peers = [(a, to) for to in others[:12]] + list(corners) + [(up_x, b), (down_x, b)] + [(a, to) for to in others[12:]]
+    for peer in peers:
+        pl.semaphore_signal(barrier, inc=1, device_id=peer, device_id_type=MESH)
 
     loads = []
     for f, src in enumerate((p_in, c_in)):
@@ -78,14 +88,6 @@
     loads[4].start()
     for copy in loads[:4] + loads[5:]:
         copy.start()
-
-    barrier = pltpu.get_barrier_semaphore()
-    corners = ((up_x, up_y), (up_x, down_y), (down_x, up_y), (down_x, down_y))
-    peers = [(up_x, b), (down_x, b)] + list(corners)
-    for k in range(1, ny):
-        peers.append((a, lax.rem(b + k, ny)))
-    for peer in peers:
-        pl.semaphore_signal(barrier, inc=1, device_id=peer, device_id_type=MESH)
 
     lane = lax.broadcasted_iota(jnp.int32, (8, LANES), 1)
     first, last = lane == 0, lane == LANES - 1
@@ -129,21 +131,17 @@
     )):
         d_copies.append(remote(pc0.at[:, :, sx, sy, :], pc0.at[:, :, dx, dy, :], d_send.at[k], d_recv.at[k], peer))
 
-    def exchange(src, dst, send, recv):
-        far, near, core = b // 8, (b // 2) % 4, b % 2
-        steps = [(df, dn, dc) for df in (1, 0) for dn in (2, 1, 3, 0) for dc in (0, 1)]
-        steps.sort(key=lambda d: -(2 * d[0] + min(d[1], 4 - d[1])))
+    def exchange(src, dst, send, recv, size):
         out = []
-        for k, (df, dn, dc) in enumerate(d for d in steps if any(d)):
-            to = ((far + df) % 2) * 8 + ((near + dn) % 4) * 2 + (core + dc) % 2
+        for k, to in enumerate(others):
             out.append(remote(
-                src.at[pl.ds(pl.multiple_of(8 * to, 8), 4), :], dst.at[pl.ds(pl.multiple_of(8 * b, 8), 4), :],
+                src.at[pl.ds(pl.multiple_of(8 * to, 8), size), :], dst.at[pl.ds(pl.multiple_of(8 * b, 8), size), :],
                 send.at[k], recv.at[k], (a, to)))
         return out
 
     here = pl.ds(pl.multiple_of(8 * b, 8), 4)
-    t_copies = exchange(s1, r1, t_send, t_recv)
-    for copy in t_copies + d_copies + x_copies + y_copies:
+    t_copies = exchange(s1, r1, t_send, t_recv, 4)
+    for copy in t_copies + y_copies + x_copies + d_copies:
         copy.start()
     r1[here, :] = s1[here, :]
     def flux(p, planes_):
@@ -242,6 +240,9 @@
             for h in range(2):
                 lat[pl.ds(pl.multiple_of(BY * group + r - RY, 8), 8), pl.ds(h * LANES, LANES)] = total[h]
 
+        rows_y = lat[pl.ds(pl.multiple_of(BY * group, BY), BY), :]
+        oy[pl.ds(pl.multiple_of(8 * group, 8), 8), :] = jnp.dot(py[...], three(rows_y, 0), preferred_element_type=jnp.float32)[:8]
+
     def late_solute(group):
         e0 = 4 * group + 4
         for r in OWN:
@@ -294,24 +295,23 @@
         flux(pc1, [(3, 17)[side] + q for q in range(4)])
         second_update((0, 3)[side], False)
 
-    on_y = jnp.dot(py[...], three(lat[...], 0), preferred_element_type=jnp.float32)
-    on_z = lax.dot_general(pz[...], three(on_y, 1), (((1,), (1,)), ((), ())), preferred_element_type=jnp.float32)
-    for z in range(4):
-        s2[pl.ds(z, 16, stride=8), pl.ds(0, 32)] = on_z[16 * z:16 * z + 16]
-    l_copies = exchange(s2, r2, l_send, l_recv)
+    on_z = lax.dot_general(pz[...], three(oy[...], 1), (((1,), (1,)), ((), ())), preferred_element_type=jnp.float32)
+    s2[pl.ds(0, 16, stride=8), :] = jnp.concatenate([on_z[16 * z:16 * z + 16] for z in range(4)], axis=1)
+    l_copies = exchange(s2, r2, l_send, l_recv, 1)
     for copy in l_copies:
         copy.start()
-    r2[here, :] = s2[here, :]
+    r2[pl.ds(pl.multiple_of(8 * b, 8), 1), :] = s2[pl.ds(pl.multiple_of(8 * b, 8), 1), :]
     lax.fori_loop(0, 2, lambda i, carry: (late_solute(3 * i), carry)[1], 0)
     for copy in l_copies:
         copy.wait_recv()
-    block = lane4 // 8
-    for x in range(4):
-        row = None
-        for s in range(16):
-            part = pltpu.roll(r2[pl.ds(8 * s, 4), :], (8 * s - 8 * x) % LANES, 1)
-            row = part if row is None else jnp.where(block == s, part, row)
-        lat_v[pl.ds(4 * x, 4), :] = row
+    sources = r2[pl.ds(0, 16, stride=8), :]
+    ahead = lax.broadcasted_iota(jnp.int32, (16, LANES), 1) // 8 - lax.broadcasted_iota(jnp.int32, (16, LANES), 0)
+    result = sources
+    for d in range(1, 16):
+        moved = pltpu.roll(pltpu.roll(sources, 8 * d, 1), 16 - d, 0)
+        result = jnp.where((ahead == d) | (ahead == d - 16), moved, result)
+    for z in range(4):
+        lat_v[pl.ds(z, 4, stride=4), :] = result[4 * z:4 * z + 4]
 
     for copy in x_copies + y_copies + d_copies + t_copies + h_copies + l_copies:
         copy.wait_send()
@@ -344,7 +344,7 @@
         out_specs=(here, here),
         scratch_shapes=[both] * 2 + [wide] * 3 + [
             pltpu.VMEM((6, 2, EY, LANES), f32),
-            pltpu.VMEM((4 * BY, 2 * LANES), f32)] + [
+            pltpu.VMEM((4 * BY, 2 * LANES), f32), pltpu.VMEM((32, 2 * LANES), f32)] + [
             pltpu.VMEM(w.shape, w.dtype) for w in weights] + [
             pltpu.VMEM((16, LANES), f32),
             pltpu.VMEM((128, LANES), f32), pltpu.VMEM((128, LANES), f32),

time: 30.7 us -> 29.9 us (0.974)
  Pallas kernels: 29.9 us -> 29.2 us
    pallas_call x1, Pallas kernels: 28.9 us -> 28.2 us  [body(): pl.pallas_call(functools.partial(kernel, nx, ny), out_shape=(pltpu.VMEM((...]
where the time goes in v6:
time: 29.9 us; the launch traced here: 29.8 us
  Pallas kernels  29.2 us (98%)
  between operations  0.64 us (2%)
    pallas_call x1, Pallas kernels, body(): pl.pallas_call(functools.partial(kernel, nx, ny), out_shape=(pltpu.VMEM((...  28.2 us
    pallas_call x1, Pallas kernels, body(): pl.pallas_call(store_kernel, out_shape=(jax.ShapeDtypeStruct(phase.shape,...  1.01 us

profile of v6, /device:TPU:1, one launch (start us, length us, event | category | flops | bytes accessed | tf_op | source)
XLA Modules:
  0.0 29.8 jit_solution(17049470123821653608)
XLA Ops:
  0.6 28.2 %substeps.1 = (f32[2,2,16,32,128]{4,3,2,1,0:T(8,128)S(1)}, f32[16,128]{1,0:T(8,128)S(1)}) custom-call(f32[16,32,256]{2,1,0:T(8,128)} %p_in.1, f32[16,32,256]{2,1,0:T(8,128)} %c_in.1, f32[16,128]{1,0:T(8,128)} %bitcast.6, bf16[384,512]{1,0:T(8,128)(2,1)} %constant.8.clone.wy_in, bf16[192,256]{1,0:T(8,128)(2,1)} %constant.9.clone.wz_in, ...), custom_call_target="tpu_custom_call" | custom-call | tf_op jit(solution)/shard_map/substeps/pallas_call | solution.py:340
  28.8 1.0 %store.1 = (f32[16,32,256]{2,1,0:T(8,128)}, f32[16,32,256]{2,1,0:T(8,128)}, f32[16,128]{1,0:T(8,128)}) custom-call(f32[2,2,16,32,128]{4,3,2,1,0:T(8,128)S(1)} %get-tuple-element.8.field, f32[16,128]{1,0:T(8,128)S(1)} %get-tuple-element.9.lat), custom_call_target="tpu_custom_call" | custom-call | tf_op jit(solution)/shard_map/store/pallas_call | solution.py:359

commit v7 on v6

--- a/solution.py
+++ b/solution.py
@@ -121,15 +121,17 @@
         x_copies.append(remote(pc0.at[:, :, src, rows, :], pc0.at[:, :, dst, rows, :], x_send.at[k], x_recv.at[k], peer))
     for k, (src, dst, peer) in enumerate(((row_hi, row_before, (a, up_y)), (row_lo, row_after, (a, down_y)))):
         y_copies.append(remote(pc0.at[:, :, planes, src, :], pc0.at[:, :, planes, dst, :], y_send.at[k], y_recv.at[k], peer))
-    first3, last3, before3, after3 = pl.ds(M, 3), pl.ds(BX + 1, 3), pl.ds(1, 3), pl.ds(M + BX, 3)
-    rows_lo, rows_hi, rows_before, rows_after = pl.ds(RY, 3), pl.ds(RY + BY - 3, 3), pl.ds(RY - 3, 3), pl.ds(RY + BY, 3)
-    for k, (sx, dx, sy, dy, peer) in enumerate((
-        (last3, before3, rows_hi, rows_before, corners[0]),
-        (last3, before3, rows_lo, rows_after, corners[1]),
-        (first3, after3, rows_hi, rows_before, corners[2]),
-        (first3, after3, rows_lo, rows_after, corners[3]),
-    )):
-        d_copies.append(remote(pc0.at[:, :, sx, sy, :], pc0.at[:, :, dx, dy, :], d_send.at[k], d_recv.at[k], peer))
+    for f, n in ((0, 3), (1, 2)):
+        low_x, high_x, before_x, after_x = pl.ds(M, n), pl.ds(M + BX - n, n), pl.ds(M - n, n), pl.ds(M + BX, n)
+        low_y, high_y, before_y, after_y = pl.ds(RY, n), pl.ds(RY + BY - n, n), pl.ds(RY - n, n), pl.ds(RY + BY, n)
+        for k, (sx, dx, sy, dy, peer) in enumerate((
+            (high_x, before_x, high_y, before_y, corners[0]),
+            (high_x, before_x, low_y, after_y, corners[1]),
+            (low_x, after_x, high_y, before_y, corners[2]),
+            (low_x, after_x, low_y, after_y, corners[3]),
+        )):
+            d_copies.append(remote(
+                pc0.at[f, :, sx, sy, :], pc0.at[f, :, dx, dy, :], d_send.at[4 * f + k], d_recv.at[4 * f + k], peer))
 
     def exchange(src, dst, send, recv, size):
         out = []
@@ -141,7 +143,7 @@
 
     here = pl.ds(pl.multiple_of(8 * b, 8), 4)
     t_copies = exchange(s1, r1, t_send, t_recv, 4)
-    for copy in t_copies + y_copies + x_copies + d_copies:
+    for copy in t_copies + y_copies + x_copies[::-1] + d_copies:
         copy.start()
     r1[here, :] = s1[here, :]
     def flux(p, planes_):
@@ -286,7 +288,7 @@
     lax.fori_loop(1, 3, lambda i, carry: (second_update(i, True), carry)[1], 0)
 
     for side in (1, 0):
-        for copy in [x_copies[side]] + d_copies[2 * side:2 * side + 2]:
+        for copy in [x_copies[side]] + d_copies[2 * side:2 * side + 2] + d_copies[4 + 2 * side:6 + 2 * side]:
             copy.wait_recv()
         flux(pc0, [(1, 19)[side] + q for q in range(4)])
         h_copies[side].wait_recv()
@@ -350,7 +352,7 @@
             pltpu.VMEM((128, LANES), f32), pltpu.VMEM((128, LANES), f32),
             pltpu.VMEM((2, 16, LANES), f32), pltpu.VMEM((2, 16, LANES), f32),
             pltpu.VMEM((128, LANES), f32), pltpu.VMEM((128, LANES), f32),
-            dma((9,)), dma((2,)), dma((2,)), dma((2,)), dma((2,)), dma((4,)), dma((4,)),
+            dma((9,)), dma((2,)), dma((2,)), dma((2,)), dma((2,)), dma((8,)), dma((8,)),
             dma((16,)), dma((16,)), dma((2,)), dma((2,)), dma((16,)), dma((16,)),
         ],
         compiler_params=pltpu.CompilerParams(collective_id=0, has_side_effects=True, vmem_limit_bytes=60 << 20),

time: 29.9 us -> 30 us (level)
  no operation moved by 1% of the time
where the time goes in v7:
time: 30 us; the launch traced here: 29.9 us
  Pallas kernels  29.3 us (98%)
  between operations  0.64 us (2%)
    pallas_call x1, Pallas kernels, body(): pl.pallas_call(functools.partial(kernel, nx, ny), out_shape=(pltpu.VMEM((...  28.2 us
    pallas_call x1, Pallas kernels, body(): pl.pallas_call(store_kernel, out_shape=(jax.ShapeDtypeStruct(phase.shape,...  1.01 us

profile of v7, /device:TPU:1, one launch (start us, length us, event | category | flops | bytes accessed | tf_op | source)
XLA Modules:
  0.0 29.9 jit_solution(12094981773735926082)
XLA Ops:
  0.6 28.2 %substeps.1 = (f32[2,2,16,32,128]{4,3,2,1,0:T(8,128)S(1)}, f32[16,128]{1,0:T(8,128)S(1)}) custom-call(f32[16,32,256]{2,1,0:T(8,128)} %p_in.1, f32[16,32,256]{2,1,0:T(8,128)} %c_in.1, f32[16,128]{1,0:T(8,128)} %bitcast.6, bf16[384,512]{1,0:T(8,128)(2,1)} %constant.8.clone.wy_in, bf16[192,256]{1,0:T(8,128)(2,1)} %constant.9.clone.wz_in, ...), custom_call_target="tpu_custom_call" | custom-call | tf_op jit(solution)/shard_map/substeps/pallas_call | solution.py:342
  28.9 1.0 %store.1 = (f32[16,32,256]{2,1,0:T(8,128)}, f32[16,32,256]{2,1,0:T(8,128)}, f32[16,128]{1,0:T(8,128)}) custom-call(f32[2,2,16,32,128]{4,3,2,1,0:T(8,128)S(1)} %get-tuple-element.8.field, f32[16,128]{1,0:T(8,128)S(1)} %get-tuple-element.9.lat), custom_call_target="tpu_custom_call" | custom-call | tf_op jit(solution)/shard_map/store/pallas_call | solution.py:361
